TPU v7x, 32 devices: a whole 2x2x4 slice. The times are simulated.
32 devices in a mesh: dp: 8 (over z, y), mp: 4 (over x, core).
Axes of the slice: x: 2, y: 2, z: 4, core: 2. Of those that a mesh axis runs over, the one named last changes fastest.
Arguments:
- acts: bfloat16 [8192, 2048], P('dp', 'mp'), may hold values from -6 to 6
- out_grads: bfloat16 [2, 28672, 2048], P(None, 'dp', 'mp'), may hold values from -0.125 to 0.125
- proj_old: float32 [2, 8192, 256], P(None, 'dp'), may hold values from -0.0625 to 0.0625
- moment_one: float32 [2, 28672, 256], P(None, 'dp', 'mp'), may hold values from -12 to 12
- moment_two: float32 [2, 28672, 256], P(None, 'dp', 'mp'), may hold values from 1 to 20
Outputs:
- proj_new: float32 [2, 8192, 256], P(None, 'dp')
- first_new: float32 [2, 28672, 256], P(None, 'dp', 'mp')
- second_new: float32 [2, 28672, 256], P(None, 'dp', 'mp')
- step_update: float32 [2, 28672, 256], P(None, 'dp', 'mp')
All inputs are finite; a program needn't handle non-finite values.
Results may differ from a plain program's by a relative error of at most 0.03.
Values may be sent and summed in bfloat16 or wider, within the bound.
A program may use at most 128 MiB of HBM per device.

v0:
```python
import jax
import jax.numpy as jnp
from jax import lax
from jax.sharding import PartitionSpec as P

SWEEPS = 2


def orthonormal(image, gram):
    lower = jnp.linalg.cholesky(gram)
    solved = jax.scipy.linalg.solve_triangular(lower, jnp.swapaxes(image, 1, 2), lower=True)
    return jnp.swapaxes(solved, 1, 2)


def shards(acts, out_grads, proj_old, moment_one, moment_two):

    def grads_fold(piece):
        return jnp.einsum("kft,tkr->kfr", out_grads, piece, preferred_element_type=jnp.float32)

    def token_product(basis):
        basis_half = basis.astype(jnp.bfloat16)
        local = jnp.einsum("dt,kdr->tkr", acts, basis_half, preferred_element_type=jnp.float32)
        share = lax.psum_scatter(local, "dp", scatter_dimension=0, tiled=True).astype(jnp.bfloat16)
        coeff = lax.all_gather(share, "dp", axis=0, tiled=True)
        return grads_fold(coeff)

    basis = proj_old
    for sweep in range(SWEEPS):
        hidden_part = token_product(basis)
        hidden_share = lax.psum_scatter(
            hidden_part.astype(jnp.bfloat16), "mp", scatter_dimension=1, tiled=True
        )
        token_part = jnp.einsum(
            "kft,kfr->tkr",
            out_grads,
            lax.all_gather(hidden_share, "mp", axis=1, tiled=True),
            preferred_element_type=jnp.float32,
        )
        token_share = lax.psum_scatter(token_part, "dp", scatter_dimension=0, tiled=True).astype(
            jnp.bfloat16
        )
        image_part = jnp.einsum(
            "dt,tkr->kdr",
            acts,
            lax.all_gather(token_share, "dp", axis=0, tiled=True),
            preferred_element_type=jnp.float32,
        )
        image = lax.psum(image_part.astype(jnp.bfloat16), "mp").astype(jnp.float32)
        gram_local = jnp.einsum("kdr,kds->krs", image, image, precision=lax.Precision.HIGHEST)
        gram = lax.psum(gram_local, "dp")
        basis = orthonormal(image, gram)
    projected_part = token_product(basis)
    projected = lax.psum_scatter(
        projected_part.astype(jnp.bfloat16), "mp", scatter_dimension=2, tiled=True
    ).astype(jnp.float32)
    first_new = 0.9 * moment_one + 0.1 * projected
    second_new = 0.999 * moment_two + 0.001 * projected * projected
    step_update = first_new / (jnp.sqrt(second_new) + 1e-08)
    return (basis, first_new, second_new, step_update)


def solution(mesh):
    placed = (
        P("dp", "mp"),
        P(None, "dp", "mp"),
        P(None, "dp", None),
        P(None, "dp", "mp"),
        P(None, "dp", "mp"),
    )
    return jax.shard_map(
        shards,
        mesh=mesh,
        in_specs=placed,
        out_specs=(
            P(None, "dp", None),
            P(None, "dp", "mp"),
            P(None, "dp", "mp"),
            P(None, "dp", "mp"),
        ),
        check_vma=False,
    )
```

profile of v0, /device:TPU:29, one launch (start us, length us, event | category | flops | bytes accessed | tf_op | source)
XLA Modules:
  0.0 1281.3 jit_solution(4463060384800956341)
XLA Ops:
  8.4 2.3 fusion.17
  11.5 58.2 %all-reduce.23 = bf16[512,2,256]{2,1,0:T(2,128)(2,1)S(1)} all-reduce(f32[512,2,256]{2,1,0:T(2,128)S(1)} %copy.67), channel_id=2, replica_groups=mesh['dp'=8,'mp'=4] {'dp'}, use_global_device_ids=true, to_apply=%region_0.0.clone | all-reduce | flops 262144 | bytes 1572864
  71.0 25.2 %all_gather.21 = bf16[512,2,256]{2,1,0:T(2,128)(2,1)S(1)} all-gather(bf16[64,2,256]{2,1,0:T(2,128)(2,1)S(1)} %dynamic-slice_convert_fusion.4), channel_id=1, replica_groups=mesh['dp'=8,'mp'=4] {'dp'}, dimensions={0}, use_global_device_ids=true | all-gather | bytes 589824 | tf_op jit(solution)/shard_map/all_gather | solution.py:24
  96.2 7.1 fusion
  103.3 9.9 copy.106
  113.2 4.5 copy.120
  117.7 60.6 %reduce-scatter.10.cloned.1.call-done = bf16[896,512]{1,0:T(8,128)(2,1)} async-done(((bf16[3584,512]{1,0:T(8,128)(2,1)}), bf16[896,512]{1,0:T(8,128)(2,1)}) %reduce-scatter.10.cloned.1.call-update) | async-done | bytes 917520
  178.4 2.4 reshape.55
  180.8 2.6 copy.107
  183.4 32.0 %all-gather.3.cloned.1.call-done = bf16[2,3584,256]{1,2,0:T(8,128)(2,1)} async-done(((bf16[2,896,256]{1,2,0:T(8,128)(2,1)}), bf16[2,3584,256]{1,2,0:T(8,128)(2,1)}) %all-gather.3.cloned.1.call-update) | async-done | bytes 3670032 | tf_op jit(solution)/shard_map/all_gather | solution.py:36
  215.4 6.2 convolution_bitcast_fusion.3
  222.3 57.7 %all-reduce.24 = bf16[512,2,256]{2,1,0:T(2,128)(2,1)S(1)} all-reduce(f32[512,2,256]{2,1,0:T(2,128)S(1)} %copy.69), channel_id=4, replica_groups=mesh['dp'=8,'mp'=4] {'dp'}, use_global_device_ids=true, to_apply=%region_2.0.clone | all-reduce | flops 262144 | bytes 1572864
  280.1 25.3 %all_gather.23 = bf16[512,2,256]{2,1,0:T(2,128)(2,1)S(1)} all-gather(bf16[64,2,256]{2,1,0:T(2,128)(2,1)S(1)} %dynamic-slice_convert_fusion.3), channel_id=1, replica_groups=mesh['dp'=8,'mp'=4] {'dp'}, dimensions={0}, use_global_device_ids=true | all-gather | bytes 589824 | tf_op jit(solution)/shard_map/all_gather | solution.py:45
  305.4 1.7 fusion.5
  307.2 53.4 %all-reduce.16.cloned.1.call-done = bf16[2,1024,256]{1,2,0:T(8,128)(2,1)} async-done(((bf16[2,1024,256]{1,2,0:T(8,128)(2,1)}), bf16[2,1024,256]{1,2,0:T(8,128)(2,1)}) %all-reduce.16.cloned.1.call-update) | async-done | bytes 1048592 | tf_op jit(solution)/shard_map/psum | solution.py:48
  360.6 2.9 fusion.43
  363.8 1.6 convert_bitcast_fusion.1
  365.4 69.4 %all-reduce.18.cloned.1.call-done = f32[2,256,256]{1,2,0:T(8,128)} async-done(((f32[2,256,256]{1,2,0:T(8,128)}), f32[2,256,256]{1,2,0:T(8,128)}) %all-reduce.18.cloned.1.call-update) | async-done | bytes 524304 | tf_op jit(solution)/shard_map/psum | solution.py:50
  437.9 23.5 %custom-call.17 = f32[2,128,128]{2,1,0:T(8,128)S(1)} custom-call(f32[2,128,128]{2,1,0:T(8,128)S(1)} %cholesky.198), custom_call_target="Cholesky" | custom-call | tf_op jit(solution)/shard_map/jit(cholesky)/cholesky | solution.py:10
  461.4 19.7 %custom-call.18 = f32[2,1,128,128]{2,3,1,0:T(8,128)S(1)} custom-call(f32[2,1,128,128]{3,2,1,0:T(8,128)S(1)} %select_bitcast_fusion.1), custom_call_target="InvertDiagBlocksLowerTriangular" | custom-call | tf_op jit(solution)/shard_map/jit(cholesky)/cholesky | solution.py:10
  481.9 2.0 constant_dynamic-update-slice_fusion.3
  483.9 2.0 convolution_subtract_fusion.3
  485.8 24.3 %custom-call.19 = f32[2,128,128]{2,1,0:T(8,128)S(1)} custom-call(f32[2,128,128]{2,1,0:T(8,128)} %convolution_subtract_fusion.3), custom_call_target="Cholesky" | custom-call | tf_op jit(solution)/shard_map/jit(cholesky)/cholesky | solution.py:10
  511.0 2.0 select_select_fusion.1
  513.7 7.3 while.4
  514.3 3.1 bitcast_dynamic-update-slice_fusion.4
  518.0 3.0 bitcast_dynamic-update-slice_fusion.4
  521.0 41.1 %custom-call.20 = f32[2,2,128,128]{2,3,1,0:T(8,128)} custom-call(f32[2,2,128,128]{3,2,1,0:T(8,128)} %bitcast.143), custom_call_target="InvertDiagBlocksLowerTriangular" | custom-call | tf_op jit(solution)/shard_map/jit(_solve_triangular)/vmap()/triangular_solve | solution.py:11
  562.2 2.0 fusion.11
  564.2 1.9 convolution_subtract_fusion.1
  568.5 58.9 %all-reduce.25 = bf16[512,2,256]{2,1,0:T(2,128)(2,1)S(1)} all-reduce(f32[512,2,256]{2,1,0:T(2,128)S(1)} %copy.79), channel_id=5, replica_groups=mesh['dp'=8,'mp'=4] {'dp'}, use_global_device_ids=true, to_apply=%region_9.0.clone | all-reduce | flops 262144 | bytes 1572864
  627.5 25.6 %all_gather.24 = bf16[512,2,256]{2,1,0:T(2,128)(2,1)S(1)} all-gather(bf16[64,2,256]{2,1,0:T(2,128)(2,1)S(1)} %dynamic-slice_convert_fusion.2), channel_id=1, replica_groups=mesh['dp'=8,'mp'=4] {'dp'}, dimensions={0}, use_global_device_ids=true | all-gather | bytes 589824 | tf_op jit(solution)/shard_map/all_gather | solution.py:24
  653.1 7.1 fusion.1
  660.2 9.9 copy.108
  670.0 4.5 copy.121
  674.6 60.6 %reduce-scatter.12.cloned.1.call-done = bf16[896,512]{1,0:T(8,128)(2,1)} async-done(((bf16[3584,512]{1,0:T(8,128)(2,1)}), bf16[896,512]{1,0:T(8,128)(2,1)}) %reduce-scatter.12.cloned.1.call-update) | async-done | bytes 917520
  735.1 2.4 reshape.57
  737.5 2.6 copy.109
  740.4 31.8 %all-gather.5.cloned.1.call-done = bf16[2,3584,256]{1,2,0:T(8,128)(2,1)} async-done(((bf16[2,896,256]{1,2,0:T(8,128)(2,1)}), bf16[2,3584,256]{1,2,0:T(8,128)(2,1)}) %all-gather.5.cloned.1.call-update) | async-done | bytes 3670032 | tf_op jit(solution)/shard_map/all_gather | solution.py:36
  772.2 6.2 convolution_bitcast_fusion.2
  779.0 57.7 %all-reduce.26 = bf16[512,2,256]{2,1,0:T(2,128)(2,1)S(1)} all-reduce(f32[512,2,256]{2,1,0:T(2,128)S(1)} %copy.81), channel_id=7, replica_groups=mesh['dp'=8,'mp'=4] {'dp'}, use_global_device_ids=true, to_apply=%region_11.0.clone | all-reduce | flops 262144 | bytes 1572864
  836.8 25.3 %all_gather.26 = bf16[512,2,256]{2,1,0:T(2,128)(2,1)S(1)} all-gather(bf16[64,2,256]{2,1,0:T(2,128)(2,1)S(1)} %dynamic-slice_convert_fusion.1), channel_id=1, replica_groups=mesh['dp'=8,'mp'=4] {'dp'}, dimensions={0}, use_global_device_ids=true | all-gather | bytes 589824 | tf_op jit(solution)/shard_map/all_gather | solution.py:45
  862.1 1.7 fusion.6
  863.9 53.5 %all-reduce.20.cloned.1.call-done = bf16[2,1024,256]{1,2,0:T(8,128)(2,1)} async-done(((bf16[2,1024,256]{1,2,0:T(8,128)(2,1)}), bf16[2,1024,256]{1,2,0:T(8,128)(2,1)}) %all-reduce.20.cloned.1.call-update) | async-done | bytes 1048592 | tf_op jit(solution)/shard_map/psum | solution.py:48
  917.4 2.9 fusion.44
  920.4 1.6 convert_bitcast_fusion
  922.0 70.1 %all-reduce.22.cloned.1.call-done = f32[2,256,256]{1,2,0:T(8,128)} async-done(((f32[2,256,256]{1,2,0:T(8,128)}), f32[2,256,256]{1,2,0:T(8,128)}) %all-reduce.22.cloned.1.call-update) | async-done | bytes 524304 | tf_op jit(solution)/shard_map/psum | solution.py:50
  994.5 23.5 %custom-call.21 = f32[2,128,128]{2,1,0:T(8,128)S(1)} custom-call(f32[2,128,128]{2,1,0:T(8,128)S(1)} %cholesky.201), custom_call_target="Cholesky" | custom-call | tf_op jit(solution)/shard_map/jit(cholesky)/cholesky | solution.py:10
  1017.9 19.7 %custom-call.22 = f32[2,1,128,128]{2,3,1,0:T(8,128)S(1)} custom-call(f32[2,1,128,128]{3,2,1,0:T(8,128)S(1)} %select_bitcast_fusion), custom_call_target="InvertDiagBlocksLowerTriangular" | custom-call | tf_op jit(solution)/shard_map/jit(cholesky)/cholesky | solution.py:10
  1038.3 23.5 %custom-call.23 = f32[2,128,128]{2,1,0:T(8,128)S(1)} custom-call(f32[2,128,128]{2,1,0:T(8,128)S(1)} %convolution_subtract_fusion.2), custom_call_target="Cholesky" | custom-call | tf_op jit(solution)/shard_map/jit(cholesky)/cholesky | solution.py:10
  1062.3 4.0 while.5
  1062.9 1.4 bitcast_dynamic-update-slice_fusion.5
  1066.3 39.5 %custom-call.24 = f32[2,2,128,128]{2,3,1,0:T(8,128)S(1)} custom-call(f32[2,2,128,128]{3,2,1,0:T(8,128)S(1)} %bitcast.142), custom_call_target="InvertDiagBlocksLowerTriangular" | custom-call | tf_op jit(solution)/shard_map/jit(_solve_triangular)/vmap()/triangular_solve | solution.py:11
  1105.8 2.3 fusion.9
  1108.1 2.2 convolution_subtract_fusion
  1111.4 1.7 convolution_bitcast_fusion
  1113.1 2.2 copy.91
  1115.3 59.1 %all-reduce.27 = bf16[512,2,256]{2,1,0:T(2,128)(2,1)} all-reduce(f32[512,2,256]{2,1,0:T(2,128)} %copy.91), channel_id=8, replica_groups=mesh['dp'=8,'mp'=4] {'dp'}, use_global_device_ids=true, to_apply=%region_14.17.clone | all-reduce | flops 262144 | bytes 1572864
  1175.3 26.1 %all_gather.27 = bf16[512,2,256]{2,1,0:T(2,128)(2,1)S(1)} all-gather(bf16[64,2,256]{2,1,0:T(2,128)(2,1)S(1)} %dynamic-slice_convert_fusion), channel_id=1, replica_groups=mesh['dp'=8,'mp'=4] {'dp'}, dimensions={0}, use_global_device_ids=true | all-gather | bytes 589824 | tf_op jit(solution)/shard_map/all_gather | solution.py:24
  1201.4 7.1 fusion.2
  1208.5 1.5 maximum_bitcast_fusion
  1210.0 3.0 copy.93
  1213.0 56.7 %reduce-scatter.8.cloned.1.call-done = bf16[2,3584,64]{1,2,0:T(8,128)(2,1)} async-done(((bf16[2,3584,256]{1,2,0:T(8,128)(2,1)}), bf16[2,3584,64]{1,2,0:T(8,128)(2,1)}) %reduce-scatter.8.cloned.1.call-update) | async-done | bytes 917520 | tf_op jit(solution)/shard_map/reduce_scatter | solution.py:53
  1269.7 4.8 add_divide_fusion
  (83 shorter events, 22.1 us)
Async XLA Ops:
  7.2 1.2 copy-start
  7.2 171.2 %reduce-scatter.10.cloned.1.call-start = ((), (), s32[]{:S(2)}) async-start(), calls=%async_computation.10 | async-start | bytes 4587520
  10.7 59.0 %copy-start.7 = (u32[32]{0:T(128)S(1)}, u32[32]{0:T(128)}, u32[]{:S(2)}) copy-start(u32[32]{0:T(128)} %constant.98) | copy-start | bytes 388
  117.7 97.7 %all-gather.3.cloned.1.call-start = ((), (), s32[]{:S(2)}) async-start(), calls=%async_computation.3 | async-start | bytes 4587520 | tf_op jit(solution)/shard_map/all_gather | solution.py:36
  183.4 177.2 %all-reduce.16.cloned.1.call-start = ((), (), s32[]{:S(2)}) async-start(), calls=%async_computation.4 | async-start | bytes 2097152 | tf_op jit(solution)/shard_map/psum | solution.py:48
  307.1 127.6 %all-reduce.18.cloned.1.call-start = ((), (), s32[]{:S(2)}) async-start(), calls=%async_computation.5 | async-start | bytes 1048576 | tf_op jit(solution)/shard_map/psum | solution.py:50
  360.6 3.2 copy-start.1
  363.5 371.6 %reduce-scatter.12.cloned.1.call-start = ((), (), s32[]{:S(2)}) async-start(), calls=%async_computation.11 | async-start | bytes 4587520
  437.1 0.8 copy-start.5
  481.9 80.3 %copy-start.3 = (f32[2,256,1024]{2,1,0:T(8,128)S(1)}, f32[2,256,1024]{2,1,0:T(8,128)}, u32[]{:S(2)}) copy-start(f32[2,256,1024]{2,1,0:T(8,128)} %convert_bitcast_fusion.1) | copy-start | bytes 6291460
  564.1 2.0 copy-start.6
  674.5 97.7 %all-gather.5.cloned.1.call-start = ((), (), s32[]{:S(2)}) async-start(), calls=%async_computation.6 | async-start | bytes 4587520 | tf_op jit(solution)/shard_map/all_gather | solution.py:36
  740.1 177.3 %all-reduce.20.cloned.1.call-start = ((), (), s32[]{:S(2)}) async-start(), calls=%async_computation.7 | async-start | bytes 2097152 | tf_op jit(solution)/shard_map/psum | solution.py:48
  863.9 128.2 %all-reduce.22.cloned.1.call-start = ((), (), s32[]{:S(2)}) async-start(), calls=%async_computation.8 | async-start | bytes 1048576 | tf_op jit(solution)/shard_map/psum | solution.py:50
  917.4 3.0 copy-start.2
  920.3 349.4 %reduce-scatter.8.cloned.1.call-start = ((), (), s32[]{:S(2)}) async-start(), calls=%async_computation.9 | async-start | bytes 4587520 | tf_op jit(solution)/shard_map/reduce_scatter | solution.py:53
  1210.0 59.7 %copy-start.4 = (f32[2,3584,64]{1,2,0:T(8,128)S(1)}, f32[2,3584,64]{1,2,0:T(8,128)}, u32[]{:S(2)}) copy-start(f32[2,3584,64]{1,2,0:T(8,128)} %param.12) | copy-start | bytes 5505028
Sparse Core Ops, SparseCore 0:
  117.8 60.5 reduce-scatter.9
  183.5 31.8 all-gather.2
  307.2 53.3 all-reduce.15
  364.5 70.2 all-reduce.17
  674.6 60.4 reduce-scatter.11
  740.3 31.9 all-gather.4
  864.0 53.3 all-reduce.19
  921.8 70.2 all-reduce.21
  1208.6 61.0 reduce-scatter.7
where the time goes:
time: 1290 us; the launch traced here: 1280 us
  waiting for transfers between devices  488 us (38%)
  blocking collectives  419 us (32%)
  other arithmetic  230 us (18%)
  local copies, waits for them, and re-layouts  65.5 us (5%)
  matrix products  62.8 us (5%)
  between operations  15.2 us (1%)
    unnamed x5, blocking collectives  292 us
    psum x2, waiting for transfers between devices, shards(): gram = lax.psum(gram_local, 'dp')  139 us
    another operation x17, other arithmetic, orthonormal(): lower = jnp.linalg.cholesky(gram)  135 us
    unnamed x11, waiting for transfers between devices  121 us
    psum x2, waiting for transfers between devices, shards(): image = lax.psum(image_part.astype(jnp.bfloat16), 'mp').astype(jnp.float32)  107 us
    another operation x6, other arithmetic, orthonormal(): jax.scipy.linalg.solve_triangular(lower, jnp.swapaxes(image, 1, 2), lower...  82.8 us
    all_gather x3, blocking collectives, token_product(): coeff = lax.all_gather(share, 'dp', axis=0, tiled=True)  76.9 us
    all_gather x2, waiting for transfers between devices, shards(): lax.all_gather(hidden_share, 'mp', axis=1, tiled=True)  63.8 us
  transfers between devices with their start and end apart: 9, of which 9 were waited for; matrix products, arithmetic and copies ran while one was open for 1% of the time, Pallas kernels for 0%

commit v1 on v0

v1 whole, which is shorter than its diff:
```python
import functools

import jax
import jax.numpy as jnp
from jax import lax
from jax.experimental import pallas as pl
from jax.experimental.pallas import tpu as pltpu
from jax.sharding import PartitionSpec as P

SWEEPS = 2
BLOCK = 32
VMEM_LIMIT = 48 << 20


def greet(peers):
    barrier = pltpu.get_barrier_semaphore()
    for peer in peers:
        pl.semaphore_signal(barrier, inc=1, device_id=peer, device_id_type=pl.DeviceIdType.MESH)
    pl.semaphore_wait(barrier, len(peers))


def remote(src, dst, send_sem, recv_sem, peer):
    return pltpu.make_async_remote_copy(
        src_ref=src,
        dst_ref=dst,
        send_sem=send_sem,
        recv_sem=recv_sem,
        device_id=peer,
        device_id_type=pl.DeviceIdType.MESH,
    )


def reduce_dp_kernel(n, x_ref, out_ref, got, send_a, recv_a, send_b, recv_b):
    me = lax.axis_index("dp")
    peers = [lax.rem(me + step, n) for step in range(1, n)]
    greet([{"dp": peer} for peer in peers])
    first = []
    for i, peer in enumerate(peers):
        copy = remote(x_ref.at[peer], got.at[i], send_a.at[i], recv_a.at[i], {"dp": peer})
        copy.start()
        first.append(copy)
    total = x_ref[me].astype(jnp.float32)
    for i, copy in enumerate(first):
        copy.wait_recv()
        total = total + got[i].astype(jnp.float32)
    out_ref[me] = total.astype(out_ref.dtype)
    second = []
    for i, peer in enumerate(peers):
        copy = remote(out_ref.at[me], out_ref.at[me], send_b.at[i], recv_b.at[i], {"dp": peer})
        copy.start()
        second.append(copy)
    for i, copy in enumerate(second):
        source = lax.rem(me + n - 1 - i, n)
        landed = out_ref.at[source]
        remote(landed, landed, send_b.at[i], recv_b.at[i], {"dp": peers[i]}).wait_recv()
    for copy in first + second:
        copy.wait_send()


def reduce_dp(n, x, collective_id):
    rows, columns = x.shape
    piece = rows // n
    out = pl.pallas_call(
        functools.partial(reduce_dp_kernel, n),
        out_shape=jax.ShapeDtypeStruct((n, piece, columns), x.dtype),
        in_specs=[pl.BlockSpec(memory_space=pltpu.VMEM)],
        out_specs=pl.BlockSpec(memory_space=pltpu.VMEM),
        scratch_shapes=[pltpu.VMEM((n - 1, piece, columns), x.dtype)]
        + [pltpu.SemaphoreType.DMA((n - 1,))] * 4,
        compiler_params=pltpu.CompilerParams(
            collective_id=collective_id, has_side_effects=True, vmem_limit_bytes=VMEM_LIMIT
        ),
        name="reduce_dp",
    )(x.reshape(n, piece, columns))
    return out.reshape(rows, columns)


def reduce_mp_kernel(chunks, scatter, x_ref, out_ref, got_a, mid, got_b, sems):
    me = lax.axis_index("mp")
    low, high = lax.rem(me, 2), me // 2
    mate = {"mp": high * 2 + 1 - low}
    across = {"mp": (1 - high) * 2 + low}
    rows = x_ref.shape[1]
    piece = rows // chunks
    width = out_ref.shape[2]
    mine = pl.ds(pl.multiple_of(high * width, 128), width) if scatter else slice(None)
    theirs = pl.ds(pl.multiple_of((1 - high) * width, 128), width) if scatter else slice(None)
    greet([mate, across])
    stage_a, stage_b, stage_c = [], [], []
    for c in range(chunks):
        span = pl.ds(c * piece, piece)
        copy = remote(
            x_ref.at[1 - low, span], got_a.at[span], sems.at[0, c], sems.at[1, c], mate
        )
        copy.start()
        stage_a.append(copy)
    for c in range(chunks):
        span = pl.ds(c * piece, piece)
        stage_a[c].wait_recv()
        mid[span] = (
            x_ref[low, span].astype(jnp.float32) + got_a[span].astype(jnp.float32)
        ).astype(mid.dtype)
        copy = remote(mid.at[span, theirs], got_b.at[span], sems.at[2, c], sems.at[3, c], across)
        copy.start()
        stage_b.append(copy)
    for c in range(chunks):
        span = pl.ds(c * piece, piece)
        stage_b[c].wait_recv()
        out_ref[low, span] = (
            mid[span, mine].astype(jnp.float32) + got_b[span].astype(jnp.float32)
        ).astype(out_ref.dtype)
        copy = remote(
            out_ref.at[low, span], out_ref.at[low, span], sems.at[4, c], sems.at[5, c], mate
        )
        copy.start()
        stage_c.append(copy)
    for c in range(chunks):
        landed = out_ref.at[1 - low, pl.ds(c * piece, piece)]
        remote(landed, landed, sems.at[4, c], sems.at[5, c], mate).wait_recv()
    for copy in stage_a + stage_b + stage_c:
        copy.wait_send()


def reduce_mp(x, chunks, scatter, collective_id):
    rows, columns = x.shape
    half = rows // 2
    width = columns // 2 if scatter else columns
    out = pl.pallas_call(
        functools.partial(reduce_mp_kernel, chunks, scatter),
        out_shape=jax.ShapeDtypeStruct((2, half, width), x.dtype),
        in_specs=[pl.BlockSpec(memory_space=pltpu.VMEM)],
        out_specs=pl.BlockSpec(memory_space=pltpu.VMEM),
        scratch_shapes=[
            pltpu.VMEM((half, columns), x.dtype),
            pltpu.VMEM((half, columns), x.dtype),
            pltpu.VMEM((half, width), x.dtype),
            pltpu.SemaphoreType.DMA((6, chunks)),
        ],
        compiler_params=pltpu.CompilerParams(
            collective_id=collective_id, has_side_effects=True, vmem_limit_bytes=VMEM_LIMIT
        ),
        name="reduce_mp",
    )(x.reshape(2, half, columns))
    return out.reshape(rows, width)


def inverse_factor_kernel(gram_ref, out_ref, work):
    parts, size, _ = gram_ref.shape
    exact = functools.partial(
        lax.dot_general, precision=lax.Precision.HIGHEST, preferred_element_type=jnp.float32
    )
    row = lax.broadcasted_iota(jnp.int32, (size, size), 0)
    column = lax.broadcasted_iota(jnp.int32, (size, size), 1)
    for k in range(parts):
        work[k, :, :size] = gram_ref[k]
        work[k, :, size:] = jnp.where(row == column, 1.0, 0.0)
    small_row = lax.broadcasted_iota(jnp.int32, (BLOCK, 2 * BLOCK), 0)
    small_column = lax.broadcasted_iota(jnp.int32, (BLOCK, 2 * BLOCK), 1)
    for start in range(0, size, BLOCK):
        stop = start + BLOCK
        blocks = []
        for k in range(parts):
            corner = work[k, start:stop, start:stop]
            blocks.append(
                jnp.concatenate(
                    [corner, jnp.where(small_row == small_column, 1.0, 0.0)[:, :BLOCK]], axis=1
                )
            )
        scales = [jnp.zeros((BLOCK, 1), jnp.float32) for _ in range(parts)]
        index = lax.broadcasted_iota(jnp.int32, (BLOCK, 1), 0)
        for j in range(BLOCK):
            for k in range(parts):
                block = blocks[k]
                pivot = block[j : j + 1, j : j + 1]
                scales[k] = jnp.where(index == j, lax.rsqrt(pivot), scales[k])
                factor = jnp.where(index > j, block[:, j : j + 1], 0.0)
                blocks[k] = block - factor * (block[j : j + 1, :] * (1.0 / pivot))
        for k in range(parts):
            inverse = blocks[k][:, BLOCK:] * scales[k]
            done = exact(inverse, work[k, start:stop, :], (((1,), (0,)), ((), ())))
            out_ref[k, start:stop, :] = done[:, size:]
            if stop < size:
                below = exact(work[k, stop:, start:stop], inverse, (((1,), (1,)), ((), ())))
                work[k, stop:, :] -= exact(below, done, (((1,), (0,)), ((), ())))


def inverse_factor(gram):
    parts, size, _ = gram.shape
    return pl.pallas_call(
        inverse_factor_kernel,
        out_shape=jax.ShapeDtypeStruct(gram.shape, jnp.float32),
        in_specs=[pl.BlockSpec(memory_space=pltpu.VMEM)],
        out_specs=pl.BlockSpec(memory_space=pltpu.VMEM),
        scratch_shapes=[pltpu.VMEM((parts, size, 2 * size), jnp.float32)],
        compiler_params=pltpu.CompilerParams(vmem_limit_bytes=VMEM_LIMIT),
        name="inverse_factor",
    )(gram)


def shards(dp, acts, out_grads, proj_old, moment_one, moment_two):
    half = jnp.bfloat16
    parts, units, tokens = out_grads.shape
    features, rank = proj_old.shape[1:]
    einsum = functools.partial(jnp.einsum, preferred_element_type=jnp.float32)

    def token_product(basis):
        local = einsum("dt,kdr->ktr", acts, basis.astype(half)).astype(half)
        coeff = reduce_dp(dp, local.reshape(parts * tokens, rank), 0)
        product = einsum("kft,ktr->kfr", out_grads, coeff.reshape(parts, tokens, rank))
        return product.astype(half).reshape(parts * units, rank)

    basis = proj_old
    for sweep in range(SWEEPS):
        hidden = reduce_mp(token_product(basis), 7, False, 1).reshape(parts, units, rank)
        token_part = einsum("kft,kfr->ktr", out_grads, hidden).astype(half)
        token_image = reduce_dp(dp, token_part.reshape(parts * tokens, rank), 0)
        image_part = einsum("dt,ktr->kdr", acts, token_image.reshape(parts, tokens, rank))
        image = reduce_mp(image_part.astype(half).reshape(parts * features, rank), 4, False, 2)
        image = image.reshape(parts, features, rank)
        gram_local = einsum("kdr,kds->krs", image, image)
        gram = reduce_dp(dp, gram_local.reshape(parts * rank, rank), 3)
        inverse = inverse_factor(gram.reshape(parts, rank, rank))
        basis = jnp.einsum(
            "kdr,ksr->kds",
            image.astype(jnp.float32),
            inverse,
            precision=lax.Precision.HIGHEST,
        )
    projected = reduce_mp(token_product(basis), 7, True, 4)
    share = rank // 4
    low = lax.rem(lax.axis_index("mp"), 2)
    projected = lax.dynamic_slice_in_dim(projected, low * share, share, 1)
    projected = projected.reshape(parts, units, share).astype(jnp.float32)
    first_new = 0.9 * moment_one + 0.1 * projected
    second_new = 0.999 * moment_two + 0.001 * projected * projected
    step_update = first_new / (jnp.sqrt(second_new) + 1e-08)
    return (basis, first_new, second_new, step_update)


def solution(mesh):
    assert mesh.shape["mp"] == 4
    placed = (
        P("dp", "mp"),
        P(None, "dp", "mp"),
        P(None, "dp", None),
        P(None, "dp", "mp"),
        P(None, "dp", "mp"),
    )
    return jax.shard_map(
        functools.partial(shards, mesh.shape["dp"]),
        mesh=mesh,
        in_specs=placed,
        out_specs=(
            P(None, "dp", None),
            P(None, "dp", "mp"),
            P(None, "dp", "mp"),
            P(None, "dp", "mp"),
        ),
        check_vma=False,
    )
```

time: 1290 us -> 478 us (0.37)
  waiting for transfers between devices: 488 us -> 0 us
  Pallas kernels: 0 us -> 424 us
  blocking collectives: 419 us -> 0 us
  other arithmetic: 230 us -> 5.96 us
  local copies, waits for them, and re-layouts: 65.5 us -> 5.99 us
  matrix products: 62.8 us -> 32.2 us
  between operations: 15.2 us -> 1.33 us
    pallas_call x0 -> x14, Pallas kernels: none -> 424 us  [the longest x7 207 us: reduce_dp(): pl.pallas_call(functools.partial(reduce_dp_kernel, n), out_shape=jax.Shap...]
    unnamed x5 -> x0, blocking collectives: 292 us -> none
    psum x4 -> x0, waiting for transfers between devices: 246 us -> none  [the longest x2 139 us: shards(): gram = lax.psum(gram_local, 'dp')]
    another operation x23 -> x0, other arithmetic: 218 us -> none  [the longest x17 135 us: orthonormal(): lower = jnp.linalg.cholesky(gram)]
    all_gather x5 -> x0, blocking collectives: 127 us -> none  [the longest x3 76.9 us: token_product(): coeff = lax.all_gather(share, 'dp', axis=0, tiled=True)]
    unnamed x11 -> x0, waiting for transfers between devices: 121 us -> none
    all_gather x2 -> x0, waiting for transfers between devices: 63.8 us -> none  [shards(): lax.all_gather(hidden_share, 'mp', axis=1, tiled=True)]
    reduce_scatter x1 -> x0, waiting for transfers between devices: 56.7 us -> none  [shards(): lax.psum_scatter(projected_part.astype(jnp.bfloat16), 'mp', scatter_dimen...]
  transfers between devices with their start and end apart: 9 -> 0, of which waited for: 9 -> 0; matrix products, arithmetic and copies ran while one was open for 1% -> 0% of each run, Pallas kernels for 0% -> 0%
where the time goes in v1:
time: 478 us; the launch traced here: 470 us
  Pallas kernels  424 us (89%)
  matrix products  32.2 us (7%)
  local copies, waits for them, and re-layouts  5.99 us (1%)
  other arithmetic  5.96 us (1%)
    pallas_call x7, Pallas kernels, reduce_dp(): pl.pallas_call(functools.partial(reduce_dp_kernel, n), out_shape=jax.Shap...  207 us
    pallas_call x5, Pallas kernels, reduce_mp(): pl.pallas_call(functools.partial(reduce_mp_kernel, chunks, scatter), out_...  155 us
    pallas_call x2, Pallas kernels, inverse_factor(): pl.pallas_call(inverse_factor_kernel, out_shape=jax.ShapeDtypeStruct(gram...  61.5 us
    dot_general x3, matrix products, token_product(): einsum('kft,ktr->kfr', out_grads, coeff.reshape(parts, tokens, rank))  19.6 us

profile of v1, /device:TPU:29, one launch (start us, length us, event | category | flops | bytes accessed | tf_op | source)
XLA Modules:
  0.0 469.5 jit_solution(13678637698226497787)
XLA Ops:
  0.6 0.0 copy-start
  0.7 1.2 copy-done
  1.9 2.3 fusion.7
  4.2 0.2 copy.50
  4.4 0.0 slice-start
  4.4 29.3 %reduce_dp.7 = bf16[8,128,256]{2,1,0:T(8,128)(2,1)S(1)} custom-call(bf16[8,128,256]{2,1,0:T(8,128)(2,1)S(1)} %bitcast.78), custom_call_target="tpu_custom_call" | custom-call | tf_op jit(solution)/shard_map/reduce_dp/pallas_call | solution.py:63
  33.7 0.0 slice-start.1
  33.7 7.1 %fusion.x_ref = bf16[2,3584,256]{2,1,0:T(8,128)(2,1)} fusion(bf16[2,3584,512]{2,1,0:T(8,128)(2,1)} %param.6, bf16[2,512,256]{2,1,0:T(8,128)(2,1)S(1)} %bitcast.85), kind=kOutput, calls=%fused_computation.3 | convolution fusion | flops 1880883200 | bytes 11534336 | tf_op jit(solution)/shard_map/kft,ktr->kfr/dot_general | solution.py:209
  40.8 48.1 %reduce_mp.5 = bf16[2,3584,256]{2,1,0:T(8,128)(2,1)S(1)} custom-call(bf16[2,3584,256]{2,1,0:T(8,128)(2,1)} %fusion.x_ref), custom_call_target="tpu_custom_call" | custom-call | tf_op jit(solution)/shard_map/reduce_mp/pallas_call | solution.py:128
  89.0 0.0 slice-done
  89.0 0.0 slice-done.1
  89.0 2.1 fusion.10
  91.1 0.2 copy.54
  91.3 29.6 %reduce_dp.8 = bf16[8,128,256]{2,1,0:T(8,128)(2,1)S(1)} custom-call(bf16[8,128,256]{2,1,0:T(8,128)(2,1)S(1)} %bitcast.79), custom_call_target="tpu_custom_call" | custom-call | tf_op jit(solution)/shard_map/reduce_dp/pallas_call | solution.py:63
  121.0 0.7 fusion.5.x_ref
  121.7 17.0 %reduce_mp.6 = bf16[2,1024,256]{2,1,0:T(8,128)(2,1)S(1)} custom-call(bf16[2,1024,256]{2,1,0:T(8,128)(2,1)S(1)} %fusion.5.x_ref), custom_call_target="tpu_custom_call" | custom-call | tf_op jit(solution)/shard_map/reduce_mp/pallas_call | solution.py:128
  138.6 0.5 fusion.21
  139.2 29.6 %reduce_dp.9 = f32[8,64,256]{2,1,0:T(8,128)S(1)} custom-call(f32[8,64,256]{2,1,0:T(8,128)S(1)} %bitcast.76), custom_call_target="tpu_custom_call" | custom-call | tf_op jit(solution)/shard_map/reduce_dp/pallas_call | solution.py:63
  168.8 30.8 %inverse_factor.2 = f32[2,256,256]{2,1,0:T(8,128)S(1)} custom-call(f32[2,256,256]{2,1,0:T(8,128)S(1)} %bitcast.80), custom_call_target="tpu_custom_call" | custom-call | tf_op jit(solution)/shard_map/inverse_factor/pallas_call | solution.py:189
  199.6 1.1 convolution_convert_fusion.5
  200.7 0.7 fusion.8
  201.4 0.2 copy.59
  201.6 0.0 slice-start.2
  201.6 29.6 %reduce_dp.10 = bf16[8,128,256]{2,1,0:T(8,128)(2,1)S(1)} custom-call(bf16[8,128,256]{2,1,0:T(8,128)(2,1)S(1)} %bitcast.81), custom_call_target="tpu_custom_call" | custom-call | tf_op jit(solution)/shard_map/reduce_dp/pallas_call | solution.py:63
  231.2 0.0 slice-start.3
  231.3 7.3 %fusion.1.x_ref = bf16[2,3584,256]{2,1,0:T(8,128)(2,1)} fusion(bf16[2,3584,512]{2,1,0:T(8,128)(2,1)} %param.6, bf16[2,512,256]{2,1,0:T(8,128)(2,1)S(1)} %bitcast.87), kind=kOutput, calls=%fused_computation.4 | convolution fusion | flops 1880883200 | bytes 11534336 | tf_op jit(solution)/shard_map/kft,ktr->kfr/dot_general | solution.py:209
  238.6 47.7 %reduce_mp.7 = bf16[2,3584,256]{2,1,0:T(8,128)(2,1)S(1)} custom-call(bf16[2,3584,256]{2,1,0:T(8,128)(2,1)} %fusion.1.x_ref), custom_call_target="tpu_custom_call" | custom-call | tf_op jit(solution)/shard_map/reduce_mp/pallas_call | solution.py:128
  286.2 0.0 slice-done.2
  286.2 0.0 slice-done.3
  286.3 2.1 fusion.11
  288.4 0.2 copy.63
  288.6 29.6 %reduce_dp.11 = bf16[8,128,256]{2,1,0:T(8,128)(2,1)S(1)} custom-call(bf16[8,128,256]{2,1,0:T(8,128)(2,1)S(1)} %bitcast.82), custom_call_target="tpu_custom_call" | custom-call | tf_op jit(solution)/shard_map/reduce_dp/pallas_call | solution.py:63
  318.2 0.7 fusion.6.x_ref
  319.0 17.0 %reduce_mp.8 = bf16[2,1024,256]{2,1,0:T(8,128)(2,1)S(1)} custom-call(bf16[2,1024,256]{2,1,0:T(8,128)(2,1)S(1)} %fusion.6.x_ref), custom_call_target="tpu_custom_call" | custom-call | tf_op jit(solution)/shard_map/reduce_mp/pallas_call | solution.py:128
  335.9 0.5 fusion.22
  336.4 29.6 %reduce_dp.12 = f32[8,64,256]{2,1,0:T(8,128)S(1)} custom-call(f32[8,64,256]{2,1,0:T(8,128)S(1)} %bitcast.77), custom_call_target="tpu_custom_call" | custom-call | tf_op jit(solution)/shard_map/reduce_dp/pallas_call | solution.py:63
  366.1 30.7 %inverse_factor.3 = f32[2,256,256]{2,1,0:T(8,128)S(1)} custom-call(f32[2,256,256]{2,1,0:T(8,128)S(1)} %bitcast.83), custom_call_target="tpu_custom_call" | custom-call | tf_op jit(solution)/shard_map/inverse_factor/pallas_call | solution.py:189
  396.8 1.1 fusion.23
  397.9 0.0 copy-start.1
  397.9 1.3 copy-done.1
  399.2 0.8 fusion.9
  400.0 0.2 copy.68
  400.2 29.6 %reduce_dp.13 = bf16[8,128,256]{2,1,0:T(8,128)(2,1)S(1)} custom-call(bf16[8,128,256]{2,1,0:T(8,128)(2,1)S(1)} %bitcast.84), custom_call_target="tpu_custom_call" | custom-call | tf_op jit(solution)/shard_map/reduce_dp/pallas_call | solution.py:63
  429.8 5.2 %fusion.2.x_ref = bf16[2,3584,256]{2,1,0:T(8,128)(2,1)S(1)} fusion(bf16[2,3584,512]{2,1,0:T(8,128)(2,1)} %param.6, bf16[2,512,256]{2,1,0:T(8,128)(2,1)S(1)} %bitcast.89), kind=kOutput, calls=%fused_computation.5 | convolution fusion | flops 1880883200 | bytes 11534336 | tf_op jit(solution)/shard_map/kft,ktr->kfr/dot_general | solution.py:209
  435.0 25.8 %reduce_mp.9 = bf16[2,3584,128]{2,1,0:T(8,128)(2,1)S(1)} custom-call(bf16[2,3584,256]{2,1,0:T(8,128)(2,1)S(1)} %fusion.2.x_ref), custom_call_target="tpu_custom_call" | custom-call | tf_op jit(solution)/shard_map/reduce_mp/pallas_call | solution.py:128
  460.8 0.6 constant_dynamic-slice_fusion
  461.4 1.5 copy.92
  462.9 0.0 copy-start.2
  462.9 1.4 convert_element_type.97
  464.3 0.3 copy-done.2
  464.6 4.5 add_divide_fusion
  (2 shorter events, 0.0 us)
Async XLA Ops:
  0.6 1.2 copy-start
  4.4 84.6 %slice-start = ((s8[7340032]{0:T(1024)(128)(4,1)}), s8[4194304]{0:T(1024)(128)(4,1)S(1)}, s32[]{:S(2)}) async-start(s8[7340032]{0:T(1024)(128)(4,1)} %bitcast.91), calls=%async_computation | async-start | bytes 8388608
  33.7 55.3 %slice-start.1 = ((s8[7340032]{0:T(1024)(128)(4,1)}), s8[3145728]{0:T(1024)(128)(4,1)S(1)}, s32[]{:S(2)}) async-start(s8[7340032]{0:T(1024)(128)(4,1)} %bitcast.91), calls=%async_computation.1 | async-start | bytes 6291456
  201.6 84.6 %slice-start.2 = ((s8[7340032]{0:T(1024)(128)(4,1)}), s8[4194304]{0:T(1024)(128)(4,1)S(1)}, s32[]{:S(2)}) async-start(s8[7340032]{0:T(1024)(128)(4,1)} %bitcast.93), calls=%async_computation.2 | async-start | bytes 8388608
  231.2 55.0 %slice-start.3 = ((s8[7340032]{0:T(1024)(128)(4,1)}), s8[3145728]{0:T(1024)(128)(4,1)S(1)}, s32[]{:S(2)}) async-start(s8[7340032]{0:T(1024)(128)(4,1)} %bitcast.93), calls=%async_computation.3 | async-start | bytes 6291456
  397.9 1.3 copy-start.1
  462.9 1.8 copy-start.2

commit v2 on v1

--- a/solution.py
+++ b/solution.py
@@ -9,6 +9,7 @@
 
 SWEEPS = 2
 BLOCK = 32
+GROUP = 4
 VMEM_LIMIT = 48 << 20
 
 
@@ -144,39 +145,62 @@
     return out.reshape(rows, width)
 
 
-def inverse_factor_kernel(gram_ref, out_ref, work):
-    parts, size, _ = gram_ref.shape
+def eliminate(blocks):
+    shape = (BLOCK // 8, 8, 2 * BLOCK)
+    index = lax.broadcasted_iota(jnp.int32, shape, 0) * 8 + lax.broadcasted_iota(
+        jnp.int32, shape, 1
+    )
+    wide = (8, 2 * BLOCK)
+    blocks = [block.reshape(shape) for block in blocks]
+    scales = [jnp.zeros(shape, jnp.float32) for _ in blocks]
+    for j in range(0, BLOCK, GROUP):
+        for k, block in enumerate(blocks):
+            rows, columns, cross = [], [], []
+            for q in range(GROUP):
+                line = block[(j + q) // 8, (j + q) % 8 : (j + q) % 8 + 1, :]
+                rows.append(jnp.broadcast_to(line, wide))
+                columns.append(jnp.broadcast_to(block[:, :, j + q : j + q + 1], shape))
+                cross.append(
+                    [jnp.broadcast_to(line[:, j + s : j + s + 1], wide) for s in range(GROUP)]
+                )
+            for q in range(GROUP):
+                pivot = cross[q][q]
+                reciprocal = 1.0 / pivot
+                for s in range(q + 1, GROUP):
+                    ratio = cross[q][s] * reciprocal
+                    for u in range(s, GROUP):
+                        cross[s][u] = cross[s][u] - ratio * cross[q][u]
+                    rows[s] = rows[s] - ratio * rows[q]
+                    columns[s] = columns[s] - ratio[None] * columns[q]
+                factor = jnp.where(index > j + q, columns[q], 0.0)
+                block = block - factor * (rows[q] * reciprocal)[None]
+                scales[k] = jnp.where(index == j + q, lax.rsqrt(pivot)[None], scales[k])
+            blocks[k] = block
+    return [
+        (block * scale).reshape(BLOCK, 2 * BLOCK)[:, BLOCK:]
+        for block, scale in zip(blocks, scales)
+    ]
+
+
+def inverse_factor(out_ref, work):
+    parts, size, _ = out_ref.shape
     exact = functools.partial(
         lax.dot_general, precision=lax.Precision.HIGHEST, preferred_element_type=jnp.float32
     )
     row = lax.broadcasted_iota(jnp.int32, (size, size), 0)
     column = lax.broadcasted_iota(jnp.int32, (size, size), 1)
     for k in range(parts):
-        work[k, :, :size] = gram_ref[k]
         work[k, :, size:] = jnp.where(row == column, 1.0, 0.0)
-    small_row = lax.broadcasted_iota(jnp.int32, (BLOCK, 2 * BLOCK), 0)
-    small_column = lax.broadcasted_iota(jnp.int32, (BLOCK, 2 * BLOCK), 1)
+    small = jnp.where(row == column, 1.0, 0.0)[:BLOCK, :BLOCK]
     for start in range(0, size, BLOCK):
         stop = start + BLOCK
-        blocks = []
-        for k in range(parts):
-            corner = work[k, start:stop, start:stop]
-            blocks.append(
-                jnp.concatenate(
-                    [corner, jnp.where(small_row == small_column, 1.0, 0.0)[:, :BLOCK]], axis=1
-                )
-            )
-        scales = [jnp.zeros((BLOCK, 1), jnp.float32) for _ in range(parts)]
-        index = lax.broadcasted_iota(jnp.int32, (BLOCK, 1), 0)
-        for j in range(BLOCK):
-            for k in range(parts):
-                block = blocks[k]
-                pivot = block[j : j + 1, j : j + 1]
-                scales[k] = jnp.where(index == j, lax.rsqrt(pivot), scales[k])
-                factor = jnp.where(index > j, block[:, j : j + 1], 0.0)
-                blocks[k] = block - factor * (block[j : j + 1, :] * (1.0 / pivot))
-        for k in range(parts):
-            inverse = blocks[k][:, BLOCK:] * scales[k]
+        inverses = eliminate(
+            [
+                jnp.concatenate([work[k, start:stop, start:stop], small], axis=1)
+                for k in range(parts)
+            ]
+        )
+        for k, inverse in enumerate(inverses):
             done = exact(inverse, work[k, start:stop, :], (((1,), (0,)), ((), ())))
             out_ref[k, start:stop, :] = done[:, size:]
             if stop < size:
@@ -184,17 +208,91 @@
                 work[k, stop:, :] -= exact(below, done, (((1,), (0,)), ((), ())))
 
 
-def inverse_factor(gram):
+def settle_kernel(
+    n, gram_ref, local_ref, coeff_ref, inverse_ref, got_g, got_c, full, work, sem_g, sem_c, sem_m
+):
+    me, quarter = lax.axis_index("dp"), lax.axis_index("mp")
+    parts, size, _ = inverse_ref.shape
+    peers = [{"dp": lax.rem(me + step, n)} for step in range(1, n)]
+    beside = [{"mp": lax.rem(quarter + step, 4)} for step in range(1, 4)]
+    greet(peers + beside)
+    started = []
+
+    def send(*copy):
+        started.append(remote(*copy))
+        started[-1].start()
+
+    for i, peer in enumerate(peers):
+        send(gram_ref.at[quarter, peer["dp"]], got_g.at[i], sem_g.at[0, i], sem_g.at[1, i], peer)
+    for i, peer in enumerate(peers):
+        send(local_ref.at[peer["dp"]], got_c.at[i], sem_c.at[0, i], sem_c.at[1, i], peer)
+    total = gram_ref[quarter, me]
+    for i, peer in enumerate(peers):
+        remote(got_g.at[i], got_g.at[i], sem_g.at[0, i], sem_g.at[1, i], peer).wait_recv()
+        total = total + got_g[i]
+    full[quarter, me] = total
+    own = full.at[quarter, me]
+    for i, peer in enumerate(peers):
+        send(own, own, sem_g.at[2, i], sem_g.at[3, i], peer)
+    for i, peer in enumerate(peers):
+        landed = full.at[quarter, lax.rem(me + n - 1 - i, n)]
+        remote(landed, landed, sem_g.at[2, i], sem_g.at[3, i], peer).wait_recv()
+    for i, peer in enumerate(beside):
+        send(full.at[quarter], full.at[quarter], sem_m.at[0, i], sem_m.at[1, i], peer)
+    for i, peer in enumerate(beside):
+        landed = full.at[lax.rem(quarter + 3 - i, 4)]
+        remote(landed, landed, sem_m.at[0, i], sem_m.at[1, i], peer).wait_recv()
+    for k in range(parts):
+        work[k, :, :size] = full[2 * k : 2 * k + 2].reshape(size, size)
+    inverse_factor(inverse_ref, work)
+    total = local_ref[me]
+    for i, peer in enumerate(peers):
+        remote(got_c.at[i], got_c.at[i], sem_c.at[0, i], sem_c.at[1, i], peer).wait_recv()
+        total = total + got_c[i]
+    coeff_ref[me] = lax.dot_general(
+        total,
+        inverse_ref[me // (n // parts)],
+        (((1,), (1,)), ((), ())),
+        precision=lax.Precision.HIGHEST,
+        preferred_element_type=jnp.float32,
+    ).astype(coeff_ref.dtype)
+    own = coeff_ref.at[me]
+    for i, peer in enumerate(peers):
+        send(own, own, sem_c.at[2, i], sem_c.at[3, i], peer)
+    for i, peer in enumerate(peers):
+        landed = coeff_ref.at[lax.rem(me + n - 1 - i, n)]
+        remote(landed, landed, sem_c.at[2, i], sem_c.at[3, i], peer).wait_recv()
+    for copy in started:
+        copy.wait_send()
+
+
+def settle(n, gram, local, collective_id):
     parts, size, _ = gram.shape
-    return pl.pallas_call(
-        inverse_factor_kernel,
-        out_shape=jax.ShapeDtypeStruct(gram.shape, jnp.float32),
-        in_specs=[pl.BlockSpec(memory_space=pltpu.VMEM)],
-        out_specs=pl.BlockSpec(memory_space=pltpu.VMEM),
-        scratch_shapes=[pltpu.VMEM((parts, size, 2 * size), jnp.float32)],
-        compiler_params=pltpu.CompilerParams(vmem_limit_bytes=VMEM_LIMIT),
-        name="inverse_factor",
-    )(gram)
+    rows, columns = local.shape
+    piece, share = rows // n, parts * size // (4 * n)
+    coeff, inverse = pl.pallas_call(
+        functools.partial(settle_kernel, n),
+        out_shape=(
+            jax.ShapeDtypeStruct((n, piece, columns), jnp.bfloat16),
+            jax.ShapeDtypeStruct(gram.shape, jnp.float32),
+        ),
+        in_specs=[pl.BlockSpec(memory_space=pltpu.VMEM)] * 2,
+        out_specs=[pl.BlockSpec(memory_space=pltpu.VMEM)] * 2,
+        scratch_shapes=[
+            pltpu.VMEM((n - 1, share, size), jnp.float32),
+            pltpu.VMEM((n - 1, piece, columns), jnp.float32),
+            pltpu.VMEM((4, n, share, size), jnp.float32),
+            pltpu.VMEM((parts, size, 2 * size), jnp.float32),
+            pltpu.SemaphoreType.DMA((4, n - 1)),
+            pltpu.SemaphoreType.DMA((4, n - 1)),
+            pltpu.SemaphoreType.DMA((2, 3)),
+        ],
+        compiler_params=pltpu.CompilerParams(
+            collective_id=collective_id, has_side_effects=True, vmem_limit_bytes=VMEM_LIMIT
+        ),
+        name="settle",
+    )(gram.reshape(4, n, share, size), local.reshape(n, piece, columns))
+    return coeff.reshape(rows, columns), inverse
 
 
 def shards(dp, acts, out_grads, proj_old, moment_one, moment_two):
@@ -203,30 +301,32 @@
     features, rank = proj_old.shape[1:]
     einsum = functools.partial(jnp.einsum, preferred_element_type=jnp.float32)
 
-    def token_product(basis):
-        local = einsum("dt,kdr->ktr", acts, basis.astype(half)).astype(half)
-        coeff = reduce_dp(dp, local.reshape(parts * tokens, rank), 0)
+    def feature_product(basis_half):
+        return einsum("dt,kdr->ktr", acts, basis_half).reshape(parts * tokens, rank)
+
+    def grads_product(coeff):
         product = einsum("kft,ktr->kfr", out_grads, coeff.reshape(parts, tokens, rank))
         return product.astype(half).reshape(parts * units, rank)
 
-    basis = proj_old
-    for sweep in range(SWEEPS):
-        hidden = reduce_mp(token_product(basis), 7, False, 1).reshape(parts, units, rank)
+    def sweep(_, carried):
+        hidden = reduce_mp(grads_product(carried[0]), 7, False, 1).reshape(parts, units, rank)
         token_part = einsum("kft,kfr->ktr", out_grads, hidden).astype(half)
         token_image = reduce_dp(dp, token_part.reshape(parts * tokens, rank), 0)
         image_part = einsum("dt,ktr->kdr", acts, token_image.reshape(parts, tokens, rank))
         image = reduce_mp(image_part.astype(half).reshape(parts * features, rank), 4, False, 2)
         image = image.reshape(parts, features, rank)
-        gram_local = einsum("kdr,kds->krs", image, image)
-        gram = reduce_dp(dp, gram_local.reshape(parts * rank, rank), 3)
-        inverse = inverse_factor(gram.reshape(parts, rank, rank))
-        basis = jnp.einsum(
-            "kdr,ksr->kds",
-            image.astype(jnp.float32),
-            inverse,
-            precision=lax.Precision.HIGHEST,
+        coeff, inverse = settle(
+            dp, einsum("kdr,kds->krs", image, image), feature_product(image), 3
         )
-    projected = reduce_mp(token_product(basis), 7, True, 4)
+        return coeff, image, inverse
+
+    coeff = reduce_dp(dp, feature_product(proj_old.astype(half)).astype(half), 0)
+    empty = jnp.zeros((parts, features, rank), half), jnp.zeros((parts, rank, rank), jnp.float32)
+    coeff, image, inverse = lax.fori_loop(0, SWEEPS, sweep, (coeff, *empty))
+    basis = jnp.einsum(
+        "kdr,ksr->kds", image.astype(jnp.float32), inverse, precision=lax.Precision.HIGHEST
+    )
+    projected = reduce_mp(grads_product(coeff), 7, True, 4)
     share = rank // 4
     low = lax.rem(lax.axis_index("mp"), 2)
     projected = lax.dynamic_slice_in_dim(projected, low * share, share, 1)

time: 478 us -> 436 us (0.912); the launches traced: 470 us -> 434 us
  Pallas kernels: 424 us -> 386 us
  matrix products: 32.2 us -> 38.2 us
    pallas_call x7 -> x3, Pallas kernels: 207 us -> 86.6 us  [reduce_dp(): pl.pallas_call(functools.partial(reduce_dp_kernel, n), out_shape=jax.Shap...]
    pallas_call x2, Pallas kernels: 61.5 us -> 144 us  [settle(): pl.pallas_call(functools.partial(settle_kernel, n), out_shape=(jax.ShapeD...]
    dot_general x12, matrix products: 30.1 us -> 35.8 us  [the longest x3 19.5 us: grads_product(): einsum('kft,ktr->kfr', out_grads, coeff.reshape(parts, tokens, rank))]
where the time goes in v2:
time: 436 us; the launch traced here: 434 us
  Pallas kernels  386 us (89%)
  matrix products  38.2 us (9%)
  other arithmetic  4.77 us (1%)
    pallas_call x5, Pallas kernels, reduce_mp(): pl.pallas_call(functools.partial(reduce_mp_kernel, chunks, scatter), out_...  155 us
    pallas_call x2, Pallas kernels, settle(): pl.pallas_call(functools.partial(settle_kernel, n), out_shape=(jax.ShapeD...  144 us
    pallas_call x3, Pallas kernels, reduce_dp(): pl.pallas_call(functools.partial(reduce_dp_kernel, n), out_shape=jax.Shap...  86.6 us
    dot_general x3, matrix products, grads_product(): einsum('kft,ktr->kfr', out_grads, coeff.reshape(parts, tokens, rank))  19.5 us

profile of v2, /device:TPU:29, one launch (start us, length us, event | category | flops | bytes accessed | tf_op | source)
XLA Modules:
  0.0 434.4 jit_solution(3397013155013441839)
XLA Ops:
  0.6 2.6 fusion.7
  3.2 0.2 copy.45
  3.4 30.1 %reduce_dp.2 = bf16[8,128,256]{2,1,0:T(8,128)(2,1)} custom-call(bf16[8,128,256]{2,1,0:T(8,128)(2,1)S(1)} %bitcast.91), custom_call_target="tpu_custom_call" | custom-call | tf_op jit(solution)/shard_map/reduce_dp/pallas_call | solution.py:64
  33.5 360.4 %while.14 = (s32[]{:T(128)}, bf16[1024,256]{1,0:T(8,128)(2,1)}, bf16[2,1024,256]{2,1,0:T(8,128)(2,1)}, f32[2,256,256]{2,1,0:T(8,128)}, bf16[2,3584,512]{2,1,0:T(...) while((s32[]{:T(128)}, bf16[1024,256]{1,0:T(8,128)(2,1)}, bf16[2,1024,256]{2,1,0:T(8,128)(2,1)}, ...), condition=%wide.region_1.0_spmd, body=%wide.region_0.0_spmd.sunk | while | flops 5102895104 | bytes 67108992 | solution.py:325
  33.5 7.1 %convolution_convert_fusion.6.x_ref = bf16[2,3584,256]{2,1,0:T(8,128)(2,1)} fusion(bf16[2,3584,512]{2,1,0:T(8,128)(2,1)} %get-tuple-element.115, bf16[2,512,256]{2,1,0:T(8,128)(2,1)} %bitcast.80), kind=kOutput, calls=%fused_computation.clone.1 | convolution fusion | flops 1880883200 | bytes 11534336 | tf_op jit(solution)/shard_map/while/body/eval_jaxpr/kft,ktr->kfr/dot_general | solution.py:308
  40.6 0.0 copy-start.4
  40.6 48.3 %reduce_mp.4 = bf16[2,3584,256]{2,1,0:T(8,128)(2,1)S(1)} custom-call(bf16[2,3584,256]{2,1,0:T(8,128)(2,1)} %convolution_convert_fusion.6.x_ref), custom_call_target="tpu_custom_call" | custom-call | tf_op jit(solution)/shard_map/while/body/eval_jaxpr/reduce_mp/pallas_call | solution.py:129
  88.9 0.0 copy-done.4
  88.9 2.1 fusion.49
  91.1 0.2 copy.68
  91.3 29.6 %reduce_dp.3 = bf16[8,128,256]{2,1,0:T(8,128)(2,1)S(1)} custom-call(bf16[8,128,256]{2,1,0:T(8,128)(2,1)S(1)} %bitcast.88), custom_call_target="tpu_custom_call" | custom-call | tf_op jit(solution)/shard_map/while/body/eval_jaxpr/reduce_dp/pallas_call | solution.py:64
  120.9 1.9 fusion.50.x_ref
  122.8 17.0 %reduce_mp.5 = bf16[2,1024,256]{2,1,0:T(8,128)(2,1)S(1)} custom-call(bf16[2,1024,256]{2,1,0:T(8,128)(2,1)S(1)} %fusion.50.x_ref), custom_call_target="tpu_custom_call" | custom-call | tf_op jit(solution)/shard_map/while/body/eval_jaxpr/reduce_mp/pallas_call | solution.py:129
  139.8 0.0 copy-start
  139.8 2.3 convolution_bitcast_fusion.2
  142.2 0.3 copy.69
  142.5 0.0 copy-done
  142.5 0.5 fusion.51
  143.0 72.0 %settle.1 = (bf16[8,128,256]{2,1,0:T(8,128)(2,1)}, f32[2,256,256]{2,1,0:T(8,128)}) custom-call(f32[4,8,16,256]{3,2,1,0:T(8,128)S(1)} %bitcast.87, f32[8,128,256]{2,1,0:T(8,128)S(1)} %bitcast.86), custom_call_target="tpu_custom_call" | custom-call | tf_op jit(solution)/shard_map/while/body/eval_jaxpr/settle/pallas_call | solution.py:273
  215.0 7.1 %convolution_convert_fusion.6.x_ref = bf16[2,3584,256]{2,1,0:T(8,128)(2,1)} fusion(bf16[2,3584,512]{2,1,0:T(8,128)(2,1)} %get-tuple-element.115, bf16[2,512,256]{2,1,0:T(8,128)(2,1)} %bitcast.80), kind=kOutput, calls=%fused_computation.clone.1 | convolution fusion | flops 1880883200 | bytes 11534336 | tf_op jit(solution)/shard_map/while/body/eval_jaxpr/kft,ktr->kfr/dot_general | solution.py:308
  222.1 0.0 copy-start.4
  222.1 47.2 %reduce_mp.4 = bf16[2,3584,256]{2,1,0:T(8,128)(2,1)S(1)} custom-call(bf16[2,3584,256]{2,1,0:T(8,128)(2,1)} %convolution_convert_fusion.6.x_ref), custom_call_target="tpu_custom_call" | custom-call | tf_op jit(solution)/shard_map/while/body/eval_jaxpr/reduce_mp/pallas_call | solution.py:129
  269.4 0.0 copy-done.4
  269.4 2.1 fusion.49
  271.5 0.2 copy.68
  271.7 26.9 %reduce_dp.3 = bf16[8,128,256]{2,1,0:T(8,128)(2,1)S(1)} custom-call(bf16[8,128,256]{2,1,0:T(8,128)(2,1)S(1)} %bitcast.88), custom_call_target="tpu_custom_call" | custom-call | tf_op jit(solution)/shard_map/while/body/eval_jaxpr/reduce_dp/pallas_call | solution.py:64
  298.6 1.9 fusion.50.x_ref
  300.6 17.7 %reduce_mp.5 = bf16[2,1024,256]{2,1,0:T(8,128)(2,1)S(1)} custom-call(bf16[2,1024,256]{2,1,0:T(8,128)(2,1)S(1)} %fusion.50.x_ref), custom_call_target="tpu_custom_call" | custom-call | tf_op jit(solution)/shard_map/while/body/eval_jaxpr/reduce_mp/pallas_call | solution.py:129
  318.3 0.0 copy-start
  318.3 2.3 convolution_bitcast_fusion.2
  320.7 0.3 copy.69
  321.0 0.0 copy-done
  321.0 0.5 fusion.51
  321.5 72.2 %settle.1 = (bf16[8,128,256]{2,1,0:T(8,128)(2,1)}, f32[2,256,256]{2,1,0:T(8,128)}) custom-call(f32[4,8,16,256]{3,2,1,0:T(8,128)S(1)} %bitcast.87, f32[8,128,256]{2,1,0:T(8,128)S(1)} %bitcast.86), custom_call_target="tpu_custom_call" | custom-call | tf_op jit(solution)/shard_map/while/body/eval_jaxpr/settle/pallas_call | solution.py:273
  394.0 5.3 %fusion.4.x_ref = bf16[2,3584,256]{2,1,0:T(8,128)(2,1)S(1)} fusion(bf16[2,3584,512]{2,1,0:T(8,128)(2,1)} %get-tuple-element.118, bf16[2,512,256]{2,1,0:T(8,128)(2,1)} %bitcast.14), kind=kOutput, calls=%fused_computation.9 | convolution fusion | flops 1880883200 | bytes 11534336 | tf_op jit(solution)/shard_map/kft,ktr->kfr/dot_general | solution.py:308
  399.3 25.3 %reduce_mp.3 = bf16[2,3584,128]{2,1,0:T(8,128)(2,1)S(1)} custom-call(bf16[2,3584,256]{2,1,0:T(8,128)(2,1)S(1)} %fusion.4.x_ref), custom_call_target="tpu_custom_call" | custom-call | tf_op jit(solution)/shard_map/reduce_mp/pallas_call | solution.py:129
  424.6 0.6 constant_dynamic-slice_fusion
  425.1 0.8 copy.60
  425.9 0.0 copy-start.2
  425.9 0.1 convert_element_type.47
  426.0 1.4 copy-done.2
  427.4 0.0 copy-start.1
  427.4 0.0 copy-start.3
  427.4 4.6 %add_divide_fusion = (f32[2,3584,64]{1,2,0:T(8,128)}, f32[2,3584,64]{1,2,0:T(8,128)}, f32[2,3584,64]{1,2,0:T(8,128)}) fusion(f32[8,2,8,3584]{3,2,1,0:T(8,128)S(1)} %bitcast.92, f32[2,3584,64]{1,2,0:T(8,128)S(1)} %copy-done.2, f32[2,3584,64]{1,2,0:T(8,128)} %param.10), kind=kLoop, calls=%fused_computation.14 | loop fusion | flops 4128768 | bytes 11010048 | tf_op jit(solution)/shard_map/div | solution.py:336
  432.1 0.0 copy-done.1
  432.1 0.0 copy-done.3
  432.1 2.4 fusion.13
  (2 shorter events, 0.0 us)
Async XLA Ops:
  40.6 48.3 %copy-start.4 = (bf16[2,3584,512]{2,1,0:T(8,128)(2,1)S(1)}, bf16[2,3584,512]{2,1,0:T(8,128)(2,1)}, u32[]{:S(2)}) copy-start(bf16[2,3584,512]{2,1,0:T(8,128)(2,1)} %get-tuple-element.115) | copy-start | bytes 22020100 | tf_op jit(solution)/shard_map/while
  139.8 2.7 copy-start
  222.1 47.2 %copy-start.4 = (bf16[2,3584,512]{2,1,0:T(8,128)(2,1)S(1)}, bf16[2,3584,512]{2,1,0:T(8,128)(2,1)}, u32[]{:S(2)}) copy-start(bf16[2,3584,512]{2,1,0:T(8,128)(2,1)} %get-tuple-element.115) | copy-start | bytes 22020100 | tf_op jit(solution)/shard_map/while
  318.3 2.7 copy-start
  425.9 1.5 copy-start.2
  427.4 4.6 %copy-start.1 = (bf16[2,1024,256]{2,1,0:T(8,128)(2,1)S(1)}, bf16[2,1024,256]{2,1,0:T(8,128)(2,1)}, u32[]{:S(2)}) copy-start(bf16[2,1024,256]{2,1,0:T(8,128)(2,1)} %get-tuple-element.38) | copy-start | bytes 3145732
  427.4 4.6 %copy-start.3 = (f32[2,256,256]{2,1,0:T(8,128)S(1)}, f32[2,256,256]{2,1,0:T(8,128)}, u32[]{:S(2)}) copy-start(f32[2,256,256]{2,1,0:T(8,128)} %get-tuple-element.39) | copy-start | bytes 1572868

commit v3 on v2

--- a/solution.py
+++ b/solution.py
@@ -8,7 +8,7 @@
 from jax.sharding import PartitionSpec as P
 
 SWEEPS = 2
-BLOCK = 32
+BLOCK = 64
 GROUP = 4
 VMEM_LIMIT = 48 << 20
 
@@ -76,16 +76,13 @@
     return out.reshape(rows, columns)
 
 
-def reduce_mp_kernel(chunks, scatter, x_ref, out_ref, got_a, mid, got_b, sems):
+def reduce_mp_kernel(chunks, x_ref, out_ref, got_a, mid, got_b, sems):
     me = lax.axis_index("mp")
     low, high = lax.rem(me, 2), me // 2
     mate = {"mp": high * 2 + 1 - low}
     across = {"mp": (1 - high) * 2 + low}
     rows = x_ref.shape[1]
     piece = rows // chunks
-    width = out_ref.shape[2]
-    mine = pl.ds(pl.multiple_of(high * width, 128), width) if scatter else slice(None)
-    theirs = pl.ds(pl.multiple_of((1 - high) * width, 128), width) if scatter else slice(None)
     greet([mate, across])
     stage_a, stage_b, stage_c = [], [], []
     for c in range(chunks):
@@ -101,14 +98,14 @@
         mid[span] = (
             x_ref[low, span].astype(jnp.float32) + got_a[span].astype(jnp.float32)
         ).astype(mid.dtype)
-        copy = remote(mid.at[span, theirs], got_b.at[span], sems.at[2, c], sems.at[3, c], across)
+        copy = remote(mid.at[span], got_b.at[span], sems.at[2, c], sems.at[3, c], across)
         copy.start()
         stage_b.append(copy)
     for c in range(chunks):
         span = pl.ds(c * piece, piece)
         stage_b[c].wait_recv()
         out_ref[low, span] = (
-            mid[span, mine].astype(jnp.float32) + got_b[span].astype(jnp.float32)
+            mid[span].astype(jnp.float32) + got_b[span].astype(jnp.float32)
         ).astype(out_ref.dtype)
         copy = remote(
             out_ref.at[low, span], out_ref.at[low, span], sems.at[4, c], sems.at[5, c], mate
@@ -122,19 +119,18 @@
         copy.wait_send()
 
 
-def reduce_mp(x, chunks, scatter, collective_id):
+def reduce_mp(x, chunks, collective_id):
     rows, columns = x.shape
     half = rows // 2
-    width = columns // 2 if scatter else columns
     out = pl.pallas_call(
-        functools.partial(reduce_mp_kernel, chunks, scatter),
-        out_shape=jax.ShapeDtypeStruct((2, half, width), x.dtype),
+        functools.partial(reduce_mp_kernel, chunks),
+        out_shape=jax.ShapeDtypeStruct((2, half, columns), x.dtype),
         in_specs=[pl.BlockSpec(memory_space=pltpu.VMEM)],
         out_specs=pl.BlockSpec(memory_space=pltpu.VMEM),
         scratch_shapes=[
             pltpu.VMEM((half, columns), x.dtype),
             pltpu.VMEM((half, columns), x.dtype),
-            pltpu.VMEM((half, width), x.dtype),
+            pltpu.VMEM((half, columns), x.dtype),
             pltpu.SemaphoreType.DMA((6, chunks)),
         ],
         compiler_params=pltpu.CompilerParams(
@@ -142,7 +138,148 @@
         ),
         name="reduce_mp",
     )(x.reshape(2, half, columns))
-    return out.reshape(rows, width)
+    return out.reshape(rows, columns)
+
+
+def hidden_kernel(
+    chunks, scatter, grads_ref, coeff_ref, out_ref, grads, sent, own, got_a, mid, got_b, hidden,
+    total, load_sem, sems
+):
+    me = lax.axis_index("mp")
+    low, high = lax.rem(me, 2), me // 2
+    mate = {"mp": high * 2 + 1 - low}
+    across = {"mp": (1 - high) * 2 + low}
+    parts, units, tokens = grads_ref.shape
+    piece = units // chunks
+    result = out_ref if scatter else hidden
+    width = result.shape[2]
+    mine = pl.ds(pl.multiple_of(high * width, 128), width) if scatter else slice(None)
+    theirs = pl.ds(pl.multiple_of((1 - high) * width, 128), width) if scatter else slice(None)
+
+    def span(c):
+        return pl.ds(pl.multiple_of(c * piece, piece), piece)
+
+    def load(c, side):
+        k = 1 - low if side == 0 else low
+        return pltpu.make_async_copy(
+            grads_ref.at[k, span(c)], grads.at[k, span(c)], load_sem.at[side, c]
+        )
+
+    def stage_a(c):
+        return remote(sent.at[span(c)], got_a.at[span(c)], sems.at[0, c], sems.at[1, c], mate)
+
+    def stage_b(c):
+        source = mid.at[span(c), theirs]
+        return remote(source, got_b.at[span(c)], sems.at[2, c], sems.at[3, c], across)
+
+    def stage_c(c, k):
+        there = result.at[k, span(c)]
+        return remote(there, there, sems.at[4, c], sems.at[5, c], mate)
+
+    def product(k, c):
+        return jnp.dot(
+            grads[k, span(c)], coeff_ref[k], preferred_element_type=jnp.float32
+        )
+
+    def image(k, c):
+        total[k] += lax.dot_general(
+            hidden[k, span(c)],
+            grads[k, span(c)],
+            (((0,), (0,)), ((), ())),
+            preferred_element_type=jnp.float32,
+        )
+
+    def loop(body):
+        lax.fori_loop(0, chunks, lambda c, _: body(c), None)
+
+    def begin(c):
+        load(c, 0).start()
+        load(c, 1).start()
+
+    def across_chunk(c):
+        stage_a(c).wait_recv()
+        mid[span(c)] = (own[span(c)] + got_a[span(c)].astype(jnp.float32)).astype(mid.dtype)
+        stage_b(c).start()
+
+    def forward(c):
+        load(c, 0).wait()
+        sent[span(c)] = product(1 - low, c).astype(sent.dtype)
+        stage_a(c).start()
+        load(c, 1).wait()
+        own[span(c)] = product(low, c)
+
+        @pl.when(c > 0)
+        def _():
+            across_chunk(c - 1)
+
+    def other(c):
+        stage_c(c, 1 - low).wait_recv()
+        if not scatter:
+            image(1 - low, c)
+
+    def backward(c):
+        stage_b(c).wait_recv()
+        result[low, span(c)] = (
+            mid[span(c), mine].astype(jnp.float32) + got_b[span(c)].astype(jnp.float32)
+        ).astype(result.dtype)
+        stage_c(c, low).start()
+        if not scatter:
+            image(low, c)
+
+        @pl.when(c > 0)
+        def _():
+            other(c - 1)
+
+    def finish(c):
+        stage_a(c).wait_send()
+        stage_b(c).wait_send()
+        stage_c(c, low).wait_send()
+
+    loop(begin)
+    if not scatter:
+        total[...] = jnp.zeros_like(total)
+    greet([mate, across])
+    loop(forward)
+    across_chunk(chunks - 1)
+    loop(backward)
+    other(chunks - 1)
+    if not scatter:
+        out_ref[...] = total[...].astype(out_ref.dtype)
+    loop(finish)
+
+
+def hidden_sums(out_grads, coeff, chunks, scatter, collective_id):
+    parts, units, tokens = out_grads.shape
+    rank = coeff.shape[2]
+    width = rank // 2 if scatter else rank
+    half = jnp.bfloat16
+    return pl.pallas_call(
+        functools.partial(hidden_kernel, chunks, scatter),
+        out_shape=jax.ShapeDtypeStruct(
+            (parts, units, width) if scatter else (parts, rank, tokens), half
+        ),
+        in_specs=[
+            pl.BlockSpec(memory_space=pl.ANY),
+            pl.BlockSpec(memory_space=pltpu.VMEM),
+        ],
+        out_specs=pl.BlockSpec(memory_space=pltpu.VMEM),
+        scratch_shapes=[
+            pltpu.VMEM(out_grads.shape, half),
+            pltpu.VMEM((units, rank), half),
+            pltpu.VMEM((units, rank), jnp.float32),
+            pltpu.VMEM((units, rank), half),
+            pltpu.VMEM((units, rank), half),
+            pltpu.VMEM((units, width), half),
+            pltpu.VMEM((8, 128) if scatter else (parts, units, rank), half),
+            pltpu.VMEM((8, 128) if scatter else (parts, rank, tokens), jnp.float32),
+            pltpu.SemaphoreType.DMA((2, chunks)),
+            pltpu.SemaphoreType.DMA((6, chunks)),
+        ],
+        compiler_params=pltpu.CompilerParams(
+            collective_id=collective_id, has_side_effects=True, vmem_limit_bytes=VMEM_LIMIT
+        ),
+        name="hidden_sums",
+    )(out_grads, coeff)
 
 
 def eliminate(blocks):
@@ -224,8 +361,6 @@
 
     for i, peer in enumerate(peers):
         send(gram_ref.at[quarter, peer["dp"]], got_g.at[i], sem_g.at[0, i], sem_g.at[1, i], peer)
-    for i, peer in enumerate(peers):
-        send(local_ref.at[peer["dp"]], got_c.at[i], sem_c.at[0, i], sem_c.at[1, i], peer)
     total = gram_ref[quarter, me]
     for i, peer in enumerate(peers):
         remote(got_g.at[i], got_g.at[i], sem_g.at[0, i], sem_g.at[1, i], peer).wait_recv()
@@ -242,6 +377,8 @@
     for i, peer in enumerate(beside):
         landed = full.at[lax.rem(quarter + 3 - i, 4)]
         remote(landed, landed, sem_m.at[0, i], sem_m.at[1, i], peer).wait_recv()
+    for i, peer in enumerate(peers):
+        send(local_ref.at[peer["dp"]], got_c.at[i], sem_c.at[0, i], sem_c.at[1, i], peer)
     for k in range(parts):
         work[k, :, :size] = full[2 * k : 2 * k + 2].reshape(size, size)
     inverse_factor(inverse_ref, work)
@@ -304,16 +441,12 @@
     def feature_product(basis_half):
         return einsum("dt,kdr->ktr", acts, basis_half).reshape(parts * tokens, rank)
 
-    def grads_product(coeff):
-        product = einsum("kft,ktr->kfr", out_grads, coeff.reshape(parts, tokens, rank))
-        return product.astype(half).reshape(parts * units, rank)
-
     def sweep(_, carried):
-        hidden = reduce_mp(grads_product(carried[0]), 7, False, 1).reshape(parts, units, rank)
-        token_part = einsum("kft,kfr->ktr", out_grads, hidden).astype(half)
-        token_image = reduce_dp(dp, token_part.reshape(parts * tokens, rank), 0)
-        image_part = einsum("dt,ktr->kdr", acts, token_image.reshape(parts, tokens, rank))
-        image = reduce_mp(image_part.astype(half).reshape(parts * features, rank), 4, False, 2)
+        coeff = carried[0].reshape(parts, tokens, rank)
+        token_part = hidden_sums(out_grads, coeff, 14, False, 1)
+        token_image = reduce_dp(dp, token_part.reshape(parts * rank, tokens), 5)
+        image_part = einsum("dt,krt->kdr", acts, token_image.reshape(parts, rank, tokens))
+        image = reduce_mp(image_part.astype(half).reshape(parts * features, rank), 4, 2)
         image = image.reshape(parts, features, rank)
         coeff, inverse = settle(
             dp, einsum("kdr,kds->krs", image, image), feature_product(image), 3
@@ -326,11 +459,11 @@
     basis = jnp.einsum(
         "kdr,ksr->kds", image.astype(jnp.float32), inverse, precision=lax.Precision.HIGHEST
     )
-    projected = reduce_mp(grads_product(coeff), 7, True, 4)
+    projected = hidden_sums(out_grads, coeff.reshape(parts, tokens, rank), 14, True, 4)
     share = rank // 4
     low = lax.rem(lax.axis_index("mp"), 2)
-    projected = lax.dynamic_slice_in_dim(projected, low * share, share, 1)
-    projected = projected.reshape(parts, units, share).astype(jnp.float32)
+    projected = lax.dynamic_slice_in_dim(projected, low * share, share, 2)
+    projected = projected.astype(jnp.float32)
     first_new = 0.9 * moment_one + 0.1 * projected
     second_new = 0.999 * moment_two + 0.001 * projected * projected
     step_update = first_new / (jnp.sqrt(second_new) + 1e-08)

time: 436 us -> 407 us (0.933)
  Pallas kernels: 386 us -> 360 us
  matrix products: 38.2 us -> 14.6 us
  local copies, waits for them, and re-layouts: 3.99 us -> 19.4 us
  other arithmetic: 4.77 us -> 9.66 us
    pallas_call x2, Pallas kernels: 144 us -> 115 us  [settle(): pl.pallas_call(functools.partial(settle_kernel, n), out_shape=(jax.ShapeD...]
    dot_general x7 -> x2, matrix products: 27.5 us -> 3.93 us  [sweep(): einsum('dt,krt->kdr', acts, token_image.reshape(parts, rank, tokens))]
    unnamed x7 -> x11, local copies, waits for them, and re-layouts: 2.13 us -> 18.6 us
    div x1, other arithmetic: 4.64 us -> 9.66 us  [shards(): step_update = first_new / (jnp.sqrt(second_new) + 1e-08)]
where the time goes in v3:
time: 407 us; the launch traced here: 404 us
  Pallas kernels  360 us (88%)
  local copies, waits for them, and re-layouts  19.4 us (5%)
  matrix products  14.6 us (4%)
  other arithmetic  9.66 us (2%)
    pallas_call x3, Pallas kernels, hidden_sums(): pl.pallas_call(functools.partial(hidden_kernel, chunks, scatter), out_sha...  123 us
    pallas_call x2, Pallas kernels, settle(): pl.pallas_call(functools.partial(settle_kernel, n), out_shape=(jax.ShapeD...  115 us
    pallas_call x3, Pallas kernels, reduce_dp(): pl.pallas_call(functools.partial(reduce_dp_kernel, n), out_shape=jax.Shap...  86.8 us
    pallas_call x2, Pallas kernels, reduce_mp(): pl.pallas_call(functools.partial(reduce_mp_kernel, chunks), out_shape=jax...  35.1 us
    unnamed x11, local copies, waits for them, and re-layouts  18.6 us
    div x1, other arithmetic, shards(): step_update = first_new / (jnp.sqrt(second_new) + 1e-08)  9.66 us

profile of v3, /device:TPU:29, one launch (start us, length us, event | category | flops | bytes accessed | tf_op | source)
XLA Modules:
  0.0 404.4 jit_solution(13401301464803919940)
XLA Ops:
  0.6 2.6 fusion.5
  3.2 0.2 copy.14
  3.4 29.3 %reduce_dp.2 = bf16[8,128,256]{2,1,0:T(8,128)(2,1)S(1)} custom-call(bf16[8,128,256]{2,1,0:T(8,128)(2,1)S(1)} %bitcast.61), custom_call_target="tpu_custom_call" | custom-call | tf_op jit(solution)/shard_map/reduce_dp/pallas_call | solution.py:64
  32.8 312.8 %while.14 = (s32[]{:T(128)}, bf16[1024,256]{1,0:T(8,128)(2,1)S(1)}, bf16[2,1024,256]{2,1,0:T(8,128)(2,1)}, f32[2,256,256]{2,1,0:T(8,128)}, bf16[2,3584,512]{2,1,...) while((s32[]{:T(128)}, bf16[1024,256]{1,0:T(8,128)(2,1)S(1)}, bf16[2,1024,256]{2,1,0:T(8,128)(2,1)}, ...), condition=%wide.region_1.0_spmd, body=%wide.region_0.0_spmd.sunk | while | flops 1342701568 | bytes 13631593 | solution.py:458
  32.8 47.4 %hidden_sums.3 = bf16[2,256,512]{2,1,0:T(8,128)(2,1)S(1)} custom-call(bf16[2,3584,512]{2,1,0:T(8,128)(2,1)} %get-tuple-element.115.grads_ref, bf16[2,512,256]{2,1,0:T(8,128)(2,1)S(1)} %bitcast.63), custom_call_target="tpu_custom_call" | custom-call | tf_op jit(solution)/shard_map/while/body/eval_jaxpr/hidden_sums/pallas_call | solution.py:256
  80.2 28.4 %reduce_dp.3 = bf16[8,64,512]{2,1,0:T(8,128)(2,1)S(1)} custom-call(bf16[8,64,512]{2,1,0:T(8,128)(2,1)S(1)} %bitcast.59), custom_call_target="tpu_custom_call" | custom-call | tf_op jit(solution)/shard_map/while/body/eval_jaxpr/reduce_dp/pallas_call | solution.py:64
  108.7 2.0 fusion.32.x_ref
  110.6 17.5 %reduce_mp.1 = bf16[2,1024,256]{2,1,0:T(8,128)(2,1)S(1)} custom-call(bf16[2,1024,256]{2,1,0:T(8,128)(2,1)S(1)} %fusion.32.x_ref), custom_call_target="tpu_custom_call" | custom-call | tf_op jit(solution)/shard_map/while/body/eval_jaxpr/reduce_mp/pallas_call | solution.py:125
  128.1 0.0 copy-start
  128.1 2.3 convolution_bitcast_fusion.2
  130.4 0.3 copy.25
  130.8 0.5 fusion.33
  131.3 0.0 copy-done
  131.3 57.6 %settle.1 = (bf16[8,128,256]{2,1,0:T(8,128)(2,1)S(1)}, f32[2,256,256]{2,1,0:T(8,128)}) custom-call(f32[4,8,16,256]{3,2,1,0:T(8,128)S(1)} %bitcast.58, f32[8,128,256]{2,1,0:T(8,128)S(1)} %bitcast.57), custom_call_target="tpu_custom_call" | custom-call | tf_op jit(solution)/shard_map/while/body/eval_jaxpr/settle/pallas_call | solution.py:410
  188.9 47.1 %hidden_sums.3 = bf16[2,256,512]{2,1,0:T(8,128)(2,1)S(1)} custom-call(bf16[2,3584,512]{2,1,0:T(8,128)(2,1)} %get-tuple-element.115.grads_ref, bf16[2,512,256]{2,1,0:T(8,128)(2,1)S(1)} %bitcast.63), custom_call_target="tpu_custom_call" | custom-call | tf_op jit(solution)/shard_map/while/body/eval_jaxpr/hidden_sums/pallas_call | solution.py:256
  236.1 29.1 %reduce_dp.3 = bf16[8,64,512]{2,1,0:T(8,128)(2,1)S(1)} custom-call(bf16[8,64,512]{2,1,0:T(8,128)(2,1)S(1)} %bitcast.59), custom_call_target="tpu_custom_call" | custom-call | tf_op jit(solution)/shard_map/while/body/eval_jaxpr/reduce_dp/pallas_call | solution.py:64
  265.2 2.0 fusion.32.x_ref
  267.1 17.6 %reduce_mp.1 = bf16[2,1024,256]{2,1,0:T(8,128)(2,1)S(1)} custom-call(bf16[2,1024,256]{2,1,0:T(8,128)(2,1)S(1)} %fusion.32.x_ref), custom_call_target="tpu_custom_call" | custom-call | tf_op jit(solution)/shard_map/while/body/eval_jaxpr/reduce_mp/pallas_call | solution.py:125
  284.7 0.0 copy-start
  284.7 2.3 convolution_bitcast_fusion.2
  287.1 0.3 copy.25
  287.4 0.5 fusion.33
  287.9 0.0 copy-done
  288.0 57.4 %settle.1 = (bf16[8,128,256]{2,1,0:T(8,128)(2,1)S(1)}, f32[2,256,256]{2,1,0:T(8,128)}) custom-call(f32[4,8,16,256]{3,2,1,0:T(8,128)S(1)} %bitcast.58, f32[8,128,256]{2,1,0:T(8,128)S(1)} %bitcast.57), custom_call_target="tpu_custom_call" | custom-call | tf_op jit(solution)/shard_map/while/body/eval_jaxpr/settle/pallas_call | solution.py:410
  345.6 0.0 copy-start.2
  345.6 0.8 copy-done.2
  346.4 28.2 %hidden_sums.2 = bf16[2,3584,128]{2,1,0:T(8,128)(2,1)S(1)} custom-call(bf16[2,3584,512]{2,1,0:T(8,128)(2,1)} %get-tuple-element.118, bf16[2,512,256]{2,1,0:T(8,128)(2,1)} %bitcast.65), custom_call_target="tpu_custom_call" | custom-call | tf_op jit(solution)/shard_map/hidden_sums/pallas_call | solution.py:256
  374.6 3.5 copy.15
  378.1 3.6 copy.16
  381.7 9.7 %add_divide_fusion = (f32[2,3584,64]{2,1,0:T(8,128)}, f32[2,3584,64]{2,1,0:T(8,128)}, f32[2,3584,64]{2,1,0:T(8,128)}) fusion(bf16[2,3584,128]{2,1,0:T(8,128)(2,1)S(1)} %hidden_sums.2, s32[]{:T(128)S(6)} %select_n.3, f32[2,3584,64]{2,1,0:T(8,128)} %copy.16, f32[2,3584,64]{2,1,0:T(8,128)} %copy.15), kind=kLoop, calls=%fused_computation.9 | loop fusion | flops 4587520 | bytes 10092548 | tf_op jit(solution)/shard_map/div | solution.py:469
  391.4 3.5 copy.17
  394.9 3.5 copy.18
  398.4 0.0 copy-start.1
  398.4 0.0 copy-start.3
  398.4 3.6 copy.19
  402.0 0.0 copy-done.1
  402.0 0.0 copy-done.3
  402.0 2.4 fusion.11
  (2 shorter events, 0.0 us)
Async XLA Ops:
  128.1 3.2 copy-start
  284.7 3.2 copy-start
  345.6 0.8 copy-start.2
  398.4 3.6 copy-start.1
  398.4 3.6 copy-start.3

commit v4 on v3

--- a/solution.py
+++ b/solution.py
@@ -460,10 +460,11 @@
         "kdr,ksr->kds", image.astype(jnp.float32), inverse, precision=lax.Precision.HIGHEST
     )
     projected = hidden_sums(out_grads, coeff.reshape(parts, tokens, rank), 14, True, 4)
+    projected = projected.reshape(parts * units, rank // 2)
     share = rank // 4
     low = lax.rem(lax.axis_index("mp"), 2)
-    projected = lax.dynamic_slice_in_dim(projected, low * share, share, 2)
-    projected = projected.astype(jnp.float32)
+    projected = lax.dynamic_slice_in_dim(projected, low * share, share, 1)
+    projected = projected.reshape(parts, units, share).astype(jnp.float32)
     first_new = 0.9 * moment_one + 0.1 * projected
     second_new = 0.999 * moment_two + 0.001 * projected * projected
     step_update = first_new / (jnp.sqrt(second_new) + 1e-08)

time: 407 us -> 389 us (0.956)
  local copies, waits for them, and re-layouts: 19.4 us -> 3.58 us
  other arithmetic: 9.66 us -> 4.77 us
    unnamed x11 -> x7, local copies, waits for them, and re-layouts: 18.6 us -> 2.13 us
    div x1, other arithmetic: 9.66 us -> 4.64 us  [shards(): step_update = first_new / (jnp.sqrt(second_new) + 1e-08)]
where the time goes in v4:
time: 389 us; the launch traced here: 386 us
  Pallas kernels  362 us (93%)
  matrix products  14.6 us (4%)
  other arithmetic  4.77 us (1%)
    pallas_call x3, Pallas kernels, hidden_sums(): pl.pallas_call(functools.partial(hidden_kernel, chunks, scatter), out_sha...  124 us
    pallas_call x2, Pallas kernels, settle(): pl.pallas_call(functools.partial(settle_kernel, n), out_shape=(jax.ShapeD...  116 us
    pallas_call x3, Pallas kernels, reduce_dp(): pl.pallas_call(functools.partial(reduce_dp_kernel, n), out_shape=jax.Shap...  87.6 us
    pallas_call x2, Pallas kernels, reduce_mp(): pl.pallas_call(functools.partial(reduce_mp_kernel, chunks), out_shape=jax...  34.7 us

profile of v4, /device:TPU:29, one launch (start us, length us, event | category | flops | bytes accessed | tf_op | source)
XLA Modules:
  0.0 386.5 jit_solution(13933573341010119754)
XLA Ops:
  0.6 2.6 fusion.5
  3.2 0.2 copy.32
  3.4 30.1 %reduce_dp.2 = bf16[8,128,256]{2,1,0:T(8,128)(2,1)} custom-call(bf16[8,128,256]{2,1,0:T(8,128)(2,1)S(1)} %bitcast.71), custom_call_target="tpu_custom_call" | custom-call | tf_op jit(solution)/shard_map/reduce_dp/pallas_call | solution.py:64
  33.5 315.2 %while.14 = (s32[]{:T(128)}, bf16[1024,256]{1,0:T(8,128)(2,1)}, bf16[2,1024,256]{2,1,0:T(8,128)(2,1)}, f32[2,256,256]{2,1,0:T(8,128)}, bf16[2,3584,512]{2,1,0:T(...) while((s32[]{:T(128)}, bf16[1024,256]{1,0:T(8,128)(2,1)}, bf16[2,1024,256]{2,1,0:T(8,128)(2,1)}, ...), condition=%wide.region_1.0_spmd, body=%wide.region_0.0_spmd.sunk | while | flops 1342701568 | bytes 13631593 | solution.py:458
  33.6 48.5 %hidden_sums.3 = bf16[2,256,512]{2,1,0:T(8,128)(2,1)S(1)} custom-call(bf16[2,3584,512]{2,1,0:T(8,128)(2,1)} %get-tuple-element.115.grads_ref, bf16[2,512,256]{2,1,0:T(8,128)(2,1)} %bitcast.60.coeff_ref), custom_call_target="tpu_custom_call" | custom-call | tf_op jit(solution)/shard_map/while/body/eval_jaxpr/hidden_sums/pallas_call | solution.py:256
  82.0 28.4 %reduce_dp.3 = bf16[8,64,512]{2,1,0:T(8,128)(2,1)S(1)} custom-call(bf16[8,64,512]{2,1,0:T(8,128)(2,1)S(1)} %bitcast.68), custom_call_target="tpu_custom_call" | custom-call | tf_op jit(solution)/shard_map/while/body/eval_jaxpr/reduce_dp/pallas_call | solution.py:64
  110.5 2.0 fusion.32.x_ref
  112.4 17.3 %reduce_mp.1 = bf16[2,1024,256]{2,1,0:T(8,128)(2,1)S(1)} custom-call(bf16[2,1024,256]{2,1,0:T(8,128)(2,1)S(1)} %fusion.32.x_ref), custom_call_target="tpu_custom_call" | custom-call | tf_op jit(solution)/shard_map/while/body/eval_jaxpr/reduce_mp/pallas_call | solution.py:125
  129.8 0.0 copy-start
  129.8 2.3 convolution_bitcast_fusion.2
  132.1 0.3 copy.48
  132.4 0.0 copy-done
  132.5 0.5 fusion.33
  133.0 58.0 %settle.1 = (bf16[8,128,256]{2,1,0:T(8,128)(2,1)}, f32[2,256,256]{2,1,0:T(8,128)}) custom-call(f32[4,8,16,256]{3,2,1,0:T(8,128)S(1)} %bitcast.67, f32[8,128,256]{2,1,0:T(8,128)S(1)} %bitcast.66), custom_call_target="tpu_custom_call" | custom-call | tf_op jit(solution)/shard_map/while/body/eval_jaxpr/settle/pallas_call | solution.py:410
  191.0 47.9 %hidden_sums.3 = bf16[2,256,512]{2,1,0:T(8,128)(2,1)S(1)} custom-call(bf16[2,3584,512]{2,1,0:T(8,128)(2,1)} %get-tuple-element.115.grads_ref, bf16[2,512,256]{2,1,0:T(8,128)(2,1)} %bitcast.60.coeff_ref), custom_call_target="tpu_custom_call" | custom-call | tf_op jit(solution)/shard_map/while/body/eval_jaxpr/hidden_sums/pallas_call | solution.py:256
  238.9 29.1 %reduce_dp.3 = bf16[8,64,512]{2,1,0:T(8,128)(2,1)S(1)} custom-call(bf16[8,64,512]{2,1,0:T(8,128)(2,1)S(1)} %bitcast.68), custom_call_target="tpu_custom_call" | custom-call | tf_op jit(solution)/shard_map/while/body/eval_jaxpr/reduce_dp/pallas_call | solution.py:64
  268.0 2.0 fusion.32.x_ref
  270.0 17.4 %reduce_mp.1 = bf16[2,1024,256]{2,1,0:T(8,128)(2,1)S(1)} custom-call(bf16[2,1024,256]{2,1,0:T(8,128)(2,1)S(1)} %fusion.32.x_ref), custom_call_target="tpu_custom_call" | custom-call | tf_op jit(solution)/shard_map/while/body/eval_jaxpr/reduce_mp/pallas_call | solution.py:125
  287.4 0.0 copy-start
  287.4 2.3 convolution_bitcast_fusion.2
  289.7 0.3 copy.48
  290.1 0.0 copy-done
  290.1 0.5 fusion.33
  290.6 58.0 %settle.1 = (bf16[8,128,256]{2,1,0:T(8,128)(2,1)}, f32[2,256,256]{2,1,0:T(8,128)}) custom-call(f32[4,8,16,256]{3,2,1,0:T(8,128)S(1)} %bitcast.67, f32[8,128,256]{2,1,0:T(8,128)S(1)} %bitcast.66), custom_call_target="tpu_custom_call" | custom-call | tf_op jit(solution)/shard_map/while/body/eval_jaxpr/settle/pallas_call | solution.py:410
  348.8 27.8 %hidden_sums.2 = bf16[2,3584,128]{2,1,0:T(8,128)(2,1)S(1)} custom-call(bf16[2,3584,512]{2,1,0:T(8,128)(2,1)} %get-tuple-element.118, bf16[2,512,256]{2,1,0:T(8,128)(2,1)} %bitcast.13.coeff_ref), custom_call_target="tpu_custom_call" | custom-call | tf_op jit(solution)/shard_map/hidden_sums/pallas_call | solution.py:256
  376.6 0.6 constant_dynamic-slice_fusion
  377.2 0.8 copy.41
  377.9 0.0 copy-start.2
  377.9 0.1 convert_element_type.31
  378.1 1.4 copy-done.2
  379.4 0.0 copy-start.1
  379.4 0.0 copy-start.3
  379.4 4.6 %add_divide_fusion = (f32[2,3584,64]{1,2,0:T(8,128)}, f32[2,3584,64]{1,2,0:T(8,128)}, f32[2,3584,64]{1,2,0:T(8,128)}) fusion(f32[8,2,8,3584]{3,2,1,0:T(8,128)S(1)} %bitcast.72, f32[2,3584,64]{1,2,0:T(8,128)S(1)} %copy-done.2, f32[2,3584,64]{1,2,0:T(8,128)} %param.10), kind=kLoop, calls=%fused_computation.9 | loop fusion | flops 4128768 | bytes 11010048 | tf_op jit(solution)/shard_map/div | solution.py:470
  384.1 0.0 copy-done.1
  384.1 0.0 copy-done.3
  384.1 2.4 fusion.11
  (2 shorter events, 0.0 us)
Async XLA Ops:
  129.8 2.7 copy-start
  287.4 2.7 copy-start
  377.9 1.5 copy-start.2
  379.4 4.6 %copy-start.1 = (bf16[2,1024,256]{2,1,0:T(8,128)(2,1)S(1)}, bf16[2,1024,256]{2,1,0:T(8,128)(2,1)}, u32[]{:S(2)}) copy-start(bf16[2,1024,256]{2,1,0:T(8,128)(2,1)} %get-tuple-element.38) | copy-start | bytes 3145732
  379.4 4.6 %copy-start.3 = (f32[2,256,256]{2,1,0:T(8,128)S(1)}, f32[2,256,256]{2,1,0:T(8,128)}, u32[]{:S(2)}) copy-start(f32[2,256,256]{2,1,0:T(8,128)} %get-tuple-element.39) | copy-start | bytes 1572868
